TPU v7x, 32 devices: a whole 2x2x4 slice. The times are simulated.
32 devices in a mesh: parts: 2 (over x), seq: 16 (over z, y, core).
Axes of the slice: x: 2, y: 2, z: 4, core: 2. Of those that a mesh axis runs over, the one named last changes fastest.
Arguments:
- prefix_latent: bfloat16 [61440, 512], P(('parts', 'seq')), parts along dimension 0, may hold values from -6 to 6
- block_order: int32 [480], P(('parts', 'seq')), parts along dimension 0, may hold values from 0 to 239, each once
- key_up: bfloat16 [512, 512], replicated, may hold values from -0.25 to 0.25
- value_up: bfloat16 [512, 512], replicated, may hold values from -0.25 to 0.25
- queries: bfloat16 [32, 4, 4096], P(('parts', 'seq')), parts along dimension 0, may hold values from -200 to 200
- new_keys: bfloat16 [32, 4, 512], P(('parts', 'seq')), parts along dimension 0, may hold values from -6 to 6
- new_values: bfloat16 [32, 4, 512], P(('parts', 'seq')), parts along dimension 0, may hold values from -6 to 6
- suffix_keys: bfloat16 [32, 4096, 512], P(('parts', 'seq')), parts along dimension 0, may hold values from -6 to 6
- suffix_values: bfloat16 [32, 4096, 512], P(('parts', 'seq')), parts along dimension 0, may hold values from -6 to 6
- suffix_len: int32 [32], P(('parts', 'seq')), parts along dimension 0, may hold values from 1 to 4096, 32768 in all
Outputs:
- attended: bfloat16 [32, 4, 4096], P(('parts', 'seq')), parts along dimension 0
There are 2 independent parts, one for each index of `parts`. A program takes and returns all parts, laid end to end along the dimension named above; an argument that names none is the same for every part. Nothing has to cross between parts.
Inputs may be any that keep to these rules, and one draw needn't show every extreme that they name: A request's cache holds its first suffix_len entries; some request holds exactly 4096. `block_order`: each block position appears once.
All inputs are finite; a program needn't handle non-finite values. No bound on the sum of `suffix_len` on one device may be relied on, other than what follows from the above.
Results may differ from a plain program's by a relative error of at most 0.005.
The roundings to bfloat16 on the way count: a program that leaves them out, or rounds other values in their place, can miss the bound.
Values may be sent and summed in bfloat16 or wider, within the bound.
No kernel may reach another device: no remote copies, remote signals or barrier semaphores. Data moves between devices by JAX's collectives and lax.ppermute only.
A program may use at most 128 MiB of HBM per device.

v0:
```python
import math

import jax
import jax.numpy as jnp
import numpy as np
from jax import lax
from jax.sharding import PartitionSpec as P

HD = 128
QH = 32
KVH = 4
BLK = 128
STEPS = 4
SUF = 4096


def phase_table(half):
    index = np.arange(half)
    freq = 500000.0 ** (-2.0 * index / (2 * half))
    mult = np.floor(2.0**24 * freq / (2 * np.pi)).astype(np.int64)
    return ((mult >> 12).astype(np.int32), (mult & 4095).astype(np.int32))


def rotate(values, position):
    half = values.shape[-1] // 2
    high, low = phase_table(half)
    spot = position[..., None]
    first = spot * jnp.asarray(low, dtype=jnp.int32)
    second = spot * jnp.asarray(high, dtype=jnp.int32) % 4096
    turns = (first + second * 4096) % 16777216
    angle = turns.astype(values.dtype) * (2.0 * math.pi / 16777216.0)
    cosine = jnp.cos(angle)[..., None, :]
    sine = jnp.sin(angle)[..., None, :]
    lower = values[..., :half]
    upper = values[..., half:]
    return jnp.concatenate([lower * cosine - upper * sine, upper * cosine + lower * sine], -1)


def local(
    prefix_latent,
    block_order,
    key_up,
    value_up,
    queries,
    new_keys,
    new_values,
    suffix_keys,
    suffix_values,
    suffix_len,
):
    seq_count = lax.axis_size("seq")
    pre_rows = prefix_latent.shape[0]
    prefix = pre_rows * seq_count
    req_rows = queries.shape[0]
    group = QH // KVH
    scale = 1.0 / math.sqrt(HD)
    rows = jnp.arange(pre_rows, dtype=jnp.int32)
    key_pos = jnp.repeat(block_order, BLK) * BLK + rows % BLK
    keys = jnp.dot(prefix_latent, key_up, preferred_element_type=jnp.float32).reshape(
        pre_rows, KVH, HD
    )
    keys = rotate(keys, key_pos).astype(jnp.bfloat16)
    values = (
        jnp.dot(prefix_latent, value_up, preferred_element_type=jnp.float32)
        .astype(jnp.bfloat16)
        .reshape(pre_rows, KVH, HD)
    )
    step_index = jnp.arange(STEPS, dtype=jnp.int32)
    query_pos = prefix + suffix_len[:, None] + step_index[None, :]
    query_rot = rotate(
        queries.astype(jnp.float32).reshape(req_rows, STEPS, QH, HD), query_pos
    ).astype(jnp.bfloat16)
    new_rot = rotate(
        new_keys.astype(jnp.float32).reshape(req_rows, STEPS, KVH, HD), query_pos
    ).astype(jnp.bfloat16)

    def shard_part(query_block):
        count = query_block.shape[0]
        width = query_block.shape[1]
        split = query_block.reshape(count, width, KVH, group, HD)
        scores = (
            jnp.einsum("rtkgd,pkd->rtkgp", split, keys, preferred_element_type=jnp.float32) * scale
        )
        peak = jnp.max(scores, -1)
        expo = jnp.exp(scores - peak[..., None])
        total = jnp.sum(expo, -1)
        summed = jnp.einsum(
            "rtkgp,pkd->rtkgd",
            expo.astype(jnp.bfloat16),
            values,
            preferred_element_type=jnp.float32,
        )
        part = summed / total[..., None]
        return (
            part.reshape(count, width, QH * HD),
            peak.reshape(count, width, QH),
            total.reshape(count, width, QH),
        )

    def prefix_attention(selected):
        width = selected.shape[1]
        whole = lax.all_gather(selected, "seq", axis=0, tiled=True)
        count = whole.shape[0]
        per_block = math.gcd(count, max(1, 512 // (width * QH)))
        blocks = whole.reshape(count // per_block, per_block, width, QH * HD)
        parts, peaks, totals = lax.map(shard_part, blocks)
        parts = parts.reshape(count, width, QH * HD)
        peaks = peaks.reshape(count, width, QH)
        totals = totals.reshape(count, width, QH)
        got_parts, got_peaks, got_totals = (
            lax.all_to_all(parts[:, None], "seq", split_axis=0, concat_axis=1, tiled=True),
            lax.all_to_all(peaks[:, None], "seq", split_axis=0, concat_axis=1, tiled=True),
            lax.all_to_all(totals[:, None], "seq", split_axis=0, concat_axis=1, tiled=True),
        )
        highest = jnp.max(got_peaks, 1)
        factor = got_totals * jnp.exp(got_peaks - highest[:, None])
        numer = jnp.sum(
            factor[..., None] * got_parts.reshape(req_rows, seq_count, width, QH, HD), 1
        )
        denom = jnp.sum(factor, 1)
        return (highest, numer, denom)

    flat_queries = query_rot.reshape(req_rows, STEPS, QH * HD)
    results = [prefix_attention(flat_queries[:, which : which + 1]) for which in range(STEPS)]
    highest = jnp.concatenate([entry[0] for entry in results], 1)
    numer = jnp.concatenate([entry[1] for entry in results], 1)
    denom = jnp.concatenate([entry[2] for entry in results], 1)
    split = query_rot.reshape(req_rows, STEPS, KVH, group, HD)
    cache_keys = suffix_keys.reshape(req_rows, SUF, KVH, HD)
    cache_values = suffix_values.reshape(req_rows, SUF, KVH, HD)
    cache_scores = (
        jnp.einsum("rtkgd,rpkd->rtkgp", split, cache_keys, preferred_element_type=jnp.float32)
        * scale
    )
    live = jnp.arange(SUF, dtype=jnp.int32)[None, :] < suffix_len[:, None]
    cache_scores = jnp.where(live[:, None, None, None, :], cache_scores, -jnp.inf)
    fresh_keys = new_rot.reshape(req_rows, STEPS, KVH, HD)
    fresh_values = new_values.reshape(req_rows, STEPS, KVH, HD)
    fresh_scores = (
        jnp.einsum("rtkgd,rukd->rtkgu", split, fresh_keys, preferred_element_type=jnp.float32)
        * scale
    )
    causal = step_index[:, None] >= step_index[None, :]
    fresh_scores = jnp.where(causal[None, :, None, None, :], fresh_scores, -jnp.inf)
    local_peak = jnp.maximum(jnp.max(cache_scores, -1), jnp.max(fresh_scores, -1))
    cache_exp = jnp.exp(cache_scores - local_peak[..., None])
    fresh_exp = jnp.exp(fresh_scores - local_peak[..., None])
    local_total = jnp.sum(cache_exp, -1) + jnp.sum(fresh_exp, -1)
    local_numer = jnp.einsum(
        "rtkgp,rpkd->rtkgd",
        cache_exp.astype(jnp.bfloat16),
        cache_values,
        preferred_element_type=jnp.float32,
    )
    local_numer = local_numer + jnp.einsum(
        "rtkgu,rukd->rtkgd",
        fresh_exp.astype(jnp.bfloat16),
        fresh_values,
        preferred_element_type=jnp.float32,
    )
    local_peak = local_peak.reshape(req_rows, STEPS, QH)
    local_total = local_total.reshape(req_rows, STEPS, QH)
    local_numer = local_numer.reshape(req_rows, STEPS, QH, HD)
    biggest = jnp.maximum(highest, local_peak)
    prefix_weight = jnp.exp(highest - biggest)
    local_weight = jnp.exp(local_peak - biggest)
    result = (numer * prefix_weight[..., None] + local_numer * local_weight[..., None]) / (
        denom * prefix_weight + local_total * local_weight
    )[..., None]
    return result.reshape(req_rows, STEPS, QH * HD).astype(jnp.bfloat16)


def solution(mesh):
    placed = (
        P(("parts", "seq"), None),
        P(("parts", "seq")),
        P(),
        P(),
        P(("parts", "seq"), None, None),
        P(("parts", "seq"), None, None),
        P(("parts", "seq"), None, None),
        P(("parts", "seq"), None, None),
        P(("parts", "seq"), None, None),
        P(("parts", "seq")),
    )
    return jax.shard_map(
        local,
        mesh=mesh,
        in_specs=placed,
        out_specs=P(("parts", "seq"), None, None),
        check_vma=False,
    )
```

profile of v0, /device:TPU:0, one launch (start us, length us, event | category | flops | bytes accessed | tf_op | source)
XLA Modules:
  0.0 271.2 jit_solution(17228398530204130083)
XLA Ops:
  0.8 0.8 convert_bitcast_fusion
  1.6 0.8 fusion.115
  3.2 23.8 %all_gather.12 = bf16[16,1,4096]{2,1,0:T(2,128)(2,1)S(1)} all-gather(bf16[1,1,4096]{2,1,0:T(2,128)(2,1)S(1)} %get-tuple-element.75), channel_id=1, replica_groups=mesh['parts'=2,'seq'=16] {'seq'}, dimensions={0}, use_global_device_ids=true | all-gather | bytes 139264 | tf_op jit(solution)/shard_map/all_gather | solution.py:102
  27.0 0.7 reduce.40
  27.7 2.4 fusion.127
  30.1 2.3 fusion.123
  32.5 3.7 %copy.155 = f32[1920,4,64]{2,0,1:T(8,128)} copy(f32[1920,4,64]{0,2,1:T(8,128)} %get-tuple-element.72) | data formatting | bytes 3932160
  36.1 3.7 %copy.156 = f32[1920,4,64]{2,0,1:T(8,128)} copy(f32[1920,4,64]{0,2,1:T(8,128)} %get-tuple-element.71) | data formatting | bytes 3932160
  39.9 4.3 %fusion.77 = (f32[1920,64]{1,0:T(8,128)S(1)}, f32[1920,64]{1,0:T(8,128)S(1)}) fusion(s32[64]{0:T(128)S(1)} %copy-done.20, s32[64]{0:T(128)S(1)} %copy-done.19, s32[1920]{0:T(1024)S(1)} %fusion.96), kind=kLoop, calls=%fused_computation.80 | loop fusion | flops 3440640 | bytes 991232 | tf_op jit(solution)/shard_map/cos | solution.py:32
  44.3 4.5 %subtract_convert_fusion = (bf16[1920,4,64]{2,0,1:T(8,128)(2,1)S(1)}, bf16[1920,4,64]{2,0,1:T(8,128)(2,1)S(1)}) fusion(f32[1920,4,64]{2,0,1:T(8,128)} %copy.156, f32[1920,4,64]{2,0,1:T(8,128)} %copy.155, f32[1920,64]{1,0:T(8,128)S(1)} %get-tuple-element.89, f32[1920,64]{1,0:T(8,128)S(1)} %get-tuple-element.88), kind=kLoop, calls=%fused_computation.20 | loop fusion | flops 3932160 | bytes 6881280 | tf_op jit(solution)/shard_map/convert.12
  48.7 1.1 maximum_bitcast_fusion
  49.8 0.8 bitcast_reduce_fusion.3
  51.1 1.9 copy-done.4
  53.0 0.8 fusion.11
  54.4 3.7 %all-to-all-start = ((f32[16,1,1,32]{3,2,1,0:T(1,128)}), f32[16,1,1,32]{3,2,1,0:T(1,128)S(1)}, u32[]{:S(2)}, u32[]{:S(2)}) async-start(f32[16,1,1,32]{3,2,1,0:T(1,128)} %copy.101), calls=%async_computation | async-start | bytes 16384 | tf_op jit(solution)/shard_map/all_to_all | solution.py:113
  58.1 1.3 convolution_convert_fusion
  59.4 0.8 copy-done.5
  60.2 0.8 fusion.64
  61.1 22.2 %all_gather.13 = bf16[16,1,4096]{2,1,0:T(2,128)(2,1)S(1)} all-gather(bf16[1,1,4096]{2,1,0:T(2,128)(2,1)S(1)} %get-tuple-element.85), channel_id=1, replica_groups=mesh['parts'=2,'seq'=16] {'seq'}, dimensions={0}, use_global_device_ids=true | all-gather | bytes 139264 | tf_op jit(solution)/shard_map/all_gather | solution.py:102
  83.3 0.7 reduce.41
  84.0 0.8 bitcast_reduce_fusion.2
  84.9 0.8 fusion.13
  85.6 0.8 copy-done.24
  86.4 0.8 fusion.61
  87.2 18.2 %all_gather.14 = bf16[16,1,4096]{2,1,0:T(2,128)(2,1)S(1)} all-gather(bf16[1,1,4096]{2,1,0:T(2,128)(2,1)S(1)} %get-tuple-element.84), channel_id=1, replica_groups=mesh['parts'=2,'seq'=16] {'seq'}, dimensions={0}, use_global_device_ids=true | all-gather | bytes 139264 | tf_op jit(solution)/shard_map/all_gather | solution.py:102
  105.4 0.7 reduce.42
  106.2 0.8 bitcast_reduce_fusion.1
  107.0 0.8 fusion.15
  107.8 0.8 copy-done.25
  108.5 0.8 fusion.58
  109.4 19.5 %all_gather.15 = bf16[16,1,4096]{2,1,0:T(2,128)(2,1)S(1)} all-gather(bf16[1,1,4096]{2,1,0:T(2,128)(2,1)S(1)} %get-tuple-element.76), channel_id=1, replica_groups=mesh['parts'=2,'seq'=16] {'seq'}, dimensions={0}, use_global_device_ids=true | all-gather | bytes 139264 | tf_op jit(solution)/shard_map/all_gather | solution.py:102
  129.6 0.8 bitcast_reduce_fusion
  130.4 0.8 fusion.17
  131.2 0.8 copy-done.26
  132.0 0.8 fusion.55
  133.5 6.9 %reshape.1695 = bf16[4096,4,128]{2,1,0:T(4,128)(2,1)} reshape(bf16[1,4096,512]{2,1,0:T(8,128)(2,1)} %param.23) | data formatting | bytes 8388608 | tf_op jit(solution)/shard_map/reshape.165
  140.4 3.8 %all-to-all-start.1 = ((f32[16,1,1,32]{3,2,1,0:T(1,128)}), f32[16,1,1,32]{3,2,1,0:T(1,128)S(1)}, u32[]{:S(2)}, u32[]{:S(2)}) async-start(f32[16,1,1,32]{3,2,1,0:T(1,128)} %copy.102), calls=%async_computation.1 | async-start | bytes 16384 | tf_op jit(solution)/shard_map/all_to_all | solution.py:112
  144.2 3.8 %fusion.125 = (f32[4,4,8]{2,0,1:T(4,128)S(1)}, f32[1,4,4,8,4096]{4,3,1,2,0:T(8,128)S(1)}) fusion(bf16[4096,4,128,1]{2,1,0,3:T(4,128)(2,1)} %bitcast.286, pred[4096]{0:T(1024)(128)(4,1)S(1)} %iota_compare_fusion, bf16[4,4,8,64]{3,2,1,0:T(8,128)(2,1)S(1)} %bitcast.301, bf16[4,4,8,64]{3,2,1,0:T(8,128)(2,1)S(1)} %bitcast.299), kind=kOutput, calls=%fused_computation.167 | convolution fusion | flops 135856000 | bytes 6328832 | tf_op jit(solution)/shard_map/rtkgd,rpkd->rtkgp/dot_general | solution.py:132
  148.7 1.9 all-to-all-done.1
  150.6 4.1 %all-to-all-start.3 = ((f32[16,1,1,32]{3,2,1,0:T(1,128)}), f32[16,1,1,32]{3,2,1,0:T(1,128)S(1)}, u32[]{:S(2)}, u32[]{:S(2)}) async-start(f32[16,1,1,32]{3,2,1,0:T(1,128)} %copy.107), calls=%async_computation.3 | async-start | bytes 16384 | tf_op jit(solution)/shard_map/all_to_all | solution.py:113
  155.4 5.6 %all-to-all-done.3 = f32[16,1,1,32]{3,2,1,0:T(1,128)S(1)} async-done(((f32[16,1,1,32]{3,2,1,0:T(1,128)}), f32[16,1,1,32]{3,2,1,0:T(1,128)S(1)}, u32[]{:S(2)}, u32[]{:S(2)}) %all-to-all-start.3) | async-done | bytes 2080 | tf_op jit(solution)/shard_map/all_to_all | solution.py:113
  161.0 3.5 %all-to-all-start.4 = ((f32[16,1,1,32]{3,2,1,0:T(1,128)}), f32[16,1,1,32]{3,2,1,0:T(1,128)S(1)}, u32[]{:S(2)}, u32[]{:S(2)}) async-start(f32[16,1,1,32]{3,2,1,0:T(1,128)} %copy.108), calls=%async_computation.4 | async-start | bytes 16384 | tf_op jit(solution)/shard_map/all_to_all | solution.py:112
  165.3 5.6 %all-to-all-done.4 = f32[16,1,1,32]{3,2,1,0:T(1,128)S(1)} async-done(((f32[16,1,1,32]{3,2,1,0:T(1,128)}), f32[16,1,1,32]{3,2,1,0:T(1,128)S(1)}, u32[]{:S(2)}, u32[]{:S(2)}) %all-to-all-start.4) | async-done | bytes 2080 | tf_op jit(solution)/shard_map/all_to_all | solution.py:112
  170.9 3.5 %all-to-all-start.6 = ((f32[16,1,1,32]{3,2,1,0:T(1,128)}), f32[16,1,1,32]{3,2,1,0:T(1,128)S(1)}, u32[]{:S(2)}, u32[]{:S(2)}) async-start(f32[16,1,1,32]{3,2,1,0:T(1,128)} %copy.113), calls=%async_computation.6 | async-start | bytes 16384 | tf_op jit(solution)/shard_map/all_to_all | solution.py:113
  175.1 5.6 %all-to-all-done.6 = f32[16,1,1,32]{3,2,1,0:T(1,128)S(1)} async-done(((f32[16,1,1,32]{3,2,1,0:T(1,128)}), f32[16,1,1,32]{3,2,1,0:T(1,128)S(1)}, u32[]{:S(2)}, u32[]{:S(2)}) %all-to-all-start.6) | async-done | bytes 2080 | tf_op jit(solution)/shard_map/all_to_all | solution.py:113
  181.3 3.5 %all-to-all-start.7 = ((f32[16,1,1,32]{3,2,1,0:T(1,128)}), f32[16,1,1,32]{3,2,1,0:T(1,128)S(1)}, u32[]{:S(2)}, u32[]{:S(2)}) async-start(f32[16,1,1,32]{3,2,1,0:T(1,128)} %copy.114), calls=%async_computation.7 | async-start | bytes 16384 | tf_op jit(solution)/shard_map/all_to_all | solution.py:112
  185.8 6.9 %reshape.1699 = bf16[4096,4,128]{2,1,0:T(4,128)(2,1)} reshape(bf16[1,4096,512]{2,1,0:T(8,128)(2,1)} %param.24) | data formatting | bytes 8388608 | tf_op jit(solution)/shard_map/reshape.180
  192.7 6.0 %all-to-all-start.9 = ((f32[16,1,1,32]{3,2,1,0:T(1,128)}), f32[16,1,1,32]{3,2,1,0:T(1,128)S(1)}, u32[]{:S(2)}, u32[]{:S(2)}) async-start(f32[16,1,1,32]{3,2,1,0:T(1,128)} %copy.119), calls=%async_computation.9 | async-start | bytes 16384 | tf_op jit(solution)/shard_map/all_to_all | solution.py:113
  198.7 3.0 %fusion.3 = f32[4,4,8,128]{3,2,1,0:T(8,128)S(1)} fusion(bf16[4096,4,128,1]{2,1,0,3:T(4,128)(2,1)} %bitcast.285, f32[1,4,4,8,4096]{4,3,1,2,0:T(8,128)S(1)} %get-tuple-element.117, f32[4,4,8]{2,0,1:T(4,128)S(1)} %max.48), kind=kOutput, calls=%fused_computation.4 | convolution fusion | flops 135266304 | bytes 6357504 | tf_op jit(solution)/shard_map/rtkgp,rpkd->rtkgd/dot_general | solution.py:149
  202.5 2.6 all-to-all-done.9
  205.7 3.5 %all-to-all-start.10 = ((f32[16,1,1,32]{3,2,1,0:T(1,128)}), f32[16,1,1,32]{3,2,1,0:T(1,128)S(1)}, u32[]{:S(2)}, u32[]{:S(2)}) async-start(f32[16,1,1,32]{3,2,1,0:T(1,128)} %copy.120), calls=%async_computation.10 | async-start | bytes 16384 | tf_op jit(solution)/shard_map/all_to_all | solution.py:112
  209.6 0.8 copy.104
  210.4 5.1 %all-to-all-done.10 = f32[16,1,1,32]{3,2,1,0:T(1,128)S(1)} async-done(((f32[16,1,1,32]{3,2,1,0:T(1,128)}), f32[16,1,1,32]{3,2,1,0:T(1,128)S(1)}, u32[]{:S(2)}, u32[]{:S(2)}) %all-to-all-start.10) | async-done | bytes 2080 | tf_op jit(solution)/shard_map/all_to_all | solution.py:112
  215.5 3.5 %all-to-all-start.2 = ((f32[16,1,1,4096]{3,1,2,0:T(1,128)}), f32[16,1,1,4096]{3,1,2,0:T(1,128)S(1)}, u32[]{:S(2)}, u32[]{:S(2)}) async-start(f32[16,1,1,4096]{3,1,2,0:T(1,128)} %bitcast.19), calls=%async_computation.2 | async-start | bytes 524288 | tf_op jit(solution)/shard_map/all_to_all | solution.py:111
  219.1 0.8 copy.110
  219.9 0.8 copy.116
  220.7 0.8 copy.122
  222.1 7.0 %all-to-all-done.2 = f32[16,1,1,4096]{3,1,2,0:T(1,128)S(1)} async-done(((f32[16,1,1,4096]{3,1,2,0:T(1,128)}), f32[16,1,1,4096]{3,1,2,0:T(1,128)S(1)}, u32[]{:S(2)}, u32[]{:S(2)}) %all-to-all-start.2) | async-done | bytes 262176 | tf_op jit(solution)/shard_map/all_to_all | solution.py:111
  229.1 3.5 %all-to-all-start.5 = ((f32[16,1,1,4096]{3,1,2,0:T(1,128)}), f32[16,1,1,4096]{3,1,2,0:T(1,128)S(1)}, u32[]{:S(2)}, u32[]{:S(2)}) async-start(f32[16,1,1,4096]{3,1,2,0:T(1,128)} %bitcast.35), calls=%async_computation.5 | async-start | bytes 524288 | tf_op jit(solution)/shard_map/all_to_all | solution.py:111
  233.4 9.3 %all-to-all-done.5 = f32[16,1,1,4096]{3,1,2,0:T(1,128)S(1)} async-done(((f32[16,1,1,4096]{3,1,2,0:T(1,128)}), f32[16,1,1,4096]{3,1,2,0:T(1,128)S(1)}, u32[]{:S(2)}, u32[]{:S(2)}) %all-to-all-start.5) | async-done | bytes 262176 | tf_op jit(solution)/shard_map/all_to_all | solution.py:111
  242.6 3.5 %all-to-all-start.8 = ((f32[16,1,1,4096]{3,1,2,0:T(1,128)}), f32[16,1,1,4096]{3,1,2,0:T(1,128)S(1)}, u32[]{:S(2)}, u32[]{:S(2)}) async-start(f32[16,1,1,4096]{3,1,2,0:T(1,128)} %bitcast.50), calls=%async_computation.8 | async-start | bytes 524288 | tf_op jit(solution)/shard_map/all_to_all | solution.py:111
  247.6 8.6 %all-to-all-done.8 = f32[16,1,1,4096]{3,1,2,0:T(1,128)S(1)} async-done(((f32[16,1,1,4096]{3,1,2,0:T(1,128)}), f32[16,1,1,4096]{3,1,2,0:T(1,128)S(1)}, u32[]{:S(2)}, u32[]{:S(2)}) %all-to-all-start.8) | async-done | bytes 262176 | tf_op jit(solution)/shard_map/all_to_all | solution.py:111
  256.2 3.5 %all-to-all-start.11 = ((f32[16,1,1,4096]{3,1,2,0:T(1,128)}), f32[16,1,1,4096]{3,1,2,0:T(1,128)S(1)}, u32[]{:S(2)}, u32[]{:S(2)}) async-start(f32[16,1,1,4096]{3,1,2,0:T(1,128)} %bitcast.65), calls=%async_computation.11 | async-start | bytes 524288 | tf_op jit(solution)/shard_map/all_to_all | solution.py:111
  261.0 8.7 %all-to-all-done.11 = f32[16,1,1,4096]{3,1,2,0:T(1,128)S(1)} async-done(((f32[16,1,1,4096]{3,1,2,0:T(1,128)}), f32[16,1,1,4096]{3,1,2,0:T(1,128)S(1)}, u32[]{:S(2)}, u32[]{:S(2)}) %all-to-all-start.11) | async-done | bytes 262176 | tf_op jit(solution)/shard_map/all_to_all | solution.py:111
  (113 shorter events, 15.2 us)
Async XLA Ops:
  0.0 27.7 %copy-start = (bf16[1920,512]{1,0:T(8,128)(2,1)S(1)}, bf16[1920,512]{1,0:T(8,128)(2,1)}, u32[]{:S(2)}) copy-start(bf16[1920,512]{1,0:T(8,128)(2,1)} %param.16) | copy-start | bytes 5898244
  2.4 0.5 copy-start.13
  2.4 0.6 copy-start.15
  36.1 3.7 %copy-start.22 = (s32[15]{0:T(128)S(1)}, s32[15]{0:T(128)}, u32[]{:S(2)}) copy-start(s32[15]{0:T(128)} %param.17) | copy-start | bytes 184
  36.1 3.8 %copy-start.19 = (s32[64]{0:T(128)S(1)}, s32[64]{0:T(128)}, u32[]{:S(2)}) copy-start(s32[64]{0:T(128)} %constant.146.clone) | copy-start | bytes 772
  36.1 3.8 %copy-start.20 = (s32[64]{0:T(128)S(1)}, s32[64]{0:T(128)}, u32[]{:S(2)}) copy-start(s32[64]{0:T(128)} %constant.147.clone) | copy-start | bytes 772
  49.8 1.3 copy-start.2
  51.1 1.9 copy-start.4
  51.1 7.0 %copy-start.21 = (bf16[512,512]{1,0:T(8,128)(2,1)S(1)}, bf16[512,512]{1,0:T(8,128)(2,1)}, u32[]{:S(2)}) copy-start(bf16[512,512]{1,0:T(8,128)(2,1)} %param.19) | copy-start | bytes 1572868
  54.4 86.0 %all-to-all-start = ((f32[16,1,1,32]{3,2,1,0:T(1,128)}), f32[16,1,1,32]{3,2,1,0:T(1,128)S(1)}, u32[]{:S(2)}, u32[]{:S(2)}) async-start(f32[16,1,1,32]{3,2,1,0:T(1,128)} %copy.101), calls=%async_computation | async-start | bytes 16384 | tf_op jit(solution)/shard_map/all_to_all | solution.py:113
  58.1 2.1 copy-start.5
  59.4 1.7 copy-start.23
  59.4 24.6 %copy-start.3 = (bf16[1920,4,128,1]{2,0,3,1:T(8,128)(2,1)S(1)}, bf16[1920,4,128,1]{2,0,3,1:T(8,128)(2,1)}, u32[]{:S(2)}) copy-start(bf16[1920,4,128,1]{2,0,3,1:T(8,128)(2,1)} %copy-done.2) | copy-start | bytes 5898244
  84.8 1.5 copy-start.24
  86.4 20.6 %copy-start.11 = (f32[16,4,8]{0,2,1:T(8,128)}, f32[16,4,8]{0,2,1:T(8,128)S(1)}, u32[]{:S(2)}) copy-start(f32[16,4,8]{0,2,1:T(8,128)S(1)} %fusion.13) | copy-start | bytes 6148
  107.0 1.5 copy-start.25
  130.4 1.5 copy-start.26
  140.4 7.6 %copy-start.12 = (f32[16,4,8]{0,2,1:T(8,128)S(1)}, f32[16,4,8]{0,2,1:T(8,128)}, u32[]{:S(2)}) copy-start(f32[16,4,8]{0,2,1:T(8,128)} %copy-done.11) | copy-start | bytes 6148
  140.4 14.3 %copy-start.17 = (bf16[1,4,512]{2,1,0:T(4,128)(2,1)S(1)}, bf16[1,4,512]{2,1,0:T(4,128)(2,1)}, u32[]{:S(2)}) copy-start(bf16[1,4,512]{2,1,0:T(4,128)(2,1)} %param.21) | copy-start | bytes 12292
  140.4 24.1 %copy-start.14 = (f32[4,64]{1,0:T(4,128)S(1)}, f32[4,64]{1,0:T(4,128)}, u32[]{:S(2)}) copy-start(f32[4,64]{1,0:T(4,128)} %copy-done.13) | copy-start | bytes 3076
  140.4 24.1 %copy-start.16 = (f32[4,64]{1,0:T(4,128)S(1)}, f32[4,64]{1,0:T(4,128)}, u32[]{:S(2)}) copy-start(f32[4,64]{1,0:T(4,128)} %copy-done.15) | copy-start | bytes 3076
  140.4 10.2 %all-to-all-start.1 = ((f32[16,1,1,32]{3,2,1,0:T(1,128)}), f32[16,1,1,32]{3,2,1,0:T(1,128)S(1)}, u32[]{:S(2)}, u32[]{:S(2)}) async-start(f32[16,1,1,32]{3,2,1,0:T(1,128)} %copy.102), calls=%async_computation.1 | async-start | bytes 16384 | tf_op jit(solution)/shard_map/all_to_all | solution.py:112
  150.6 10.4 %all-to-all-start.3 = ((f32[16,1,1,32]{3,2,1,0:T(1,128)}), f32[16,1,1,32]{3,2,1,0:T(1,128)S(1)}, u32[]{:S(2)}, u32[]{:S(2)}) async-start(f32[16,1,1,32]{3,2,1,0:T(1,128)} %copy.107), calls=%async_computation.3 | async-start | bytes 16384 | tf_op jit(solution)/shard_map/all_to_all | solution.py:113
  161.0 23.7 %copy-start.6 = (f32[16,1,1,32]{3,2,1,0:T(1,128)}, f32[16,1,1,32]{3,2,1,0:T(1,128)S(1)}, u32[]{:S(2)}) copy-start(f32[16,1,1,32]{3,2,1,0:T(1,128)S(1)} %all-to-all-done.3) | copy-start | bytes 6148
  161.0 9.9 %all-to-all-start.4 = ((f32[16,1,1,32]{3,2,1,0:T(1,128)}), f32[16,1,1,32]{3,2,1,0:T(1,128)S(1)}, u32[]{:S(2)}, u32[]{:S(2)}) async-start(f32[16,1,1,32]{3,2,1,0:T(1,128)} %copy.108), calls=%async_computation.4 | async-start | bytes 16384 | tf_op jit(solution)/shard_map/all_to_all | solution.py:112
  170.9 9.8 %all-to-all-start.6 = ((f32[16,1,1,32]{3,2,1,0:T(1,128)}), f32[16,1,1,32]{3,2,1,0:T(1,128)S(1)}, u32[]{:S(2)}, u32[]{:S(2)}) async-start(f32[16,1,1,32]{3,2,1,0:T(1,128)} %copy.113), calls=%async_computation.6 | async-start | bytes 16384 | tf_op jit(solution)/shard_map/all_to_all | solution.py:113
  180.7 0.6 copy-start.8
  181.3 11.5 %all-to-all-start.7 = ((f32[16,1,1,32]{3,2,1,0:T(1,128)}), f32[16,1,1,32]{3,2,1,0:T(1,128)S(1)}, u32[]{:S(2)}, u32[]{:S(2)}) async-start(f32[16,1,1,32]{3,2,1,0:T(1,128)} %copy.114), calls=%async_computation.7 | async-start | bytes 16384 | tf_op jit(solution)/shard_map/all_to_all | solution.py:112
  192.7 12.3 %all-to-all-start.9 = ((f32[16,1,1,32]{3,2,1,0:T(1,128)}), f32[16,1,1,32]{3,2,1,0:T(1,128)S(1)}, u32[]{:S(2)}, u32[]{:S(2)}) async-start(f32[16,1,1,32]{3,2,1,0:T(1,128)} %copy.119), calls=%async_computation.9 | async-start | bytes 16384 | tf_op jit(solution)/shard_map/all_to_all | solution.py:113
  201.8 19.9 %copy-start.18 = (bf16[1,4,512]{2,1,0:T(4,128)(2,1)S(1)}, bf16[1,4,512]{2,1,0:T(4,128)(2,1)}, u32[]{:S(2)}) copy-start(bf16[1,4,512]{2,1,0:T(4,128)(2,1)} %param.22) | copy-start | bytes 12292
  201.8 20.3 %copy-start.7 = (f32[16,1,1,32]{3,2,1,0:T(1,128)S(1)}, f32[16,1,1,32]{3,2,1,0:T(1,128)}, u32[]{:S(2)}) copy-start(f32[16,1,1,32]{3,2,1,0:T(1,128)} %copy-done.6) | copy-start | bytes 6148
  201.8 20.3 %copy-start.9 = (f32[16,1,1,32]{3,2,1,0:T(1,128)S(1)}, f32[16,1,1,32]{3,2,1,0:T(1,128)}, u32[]{:S(2)}) copy-start(f32[16,1,1,32]{3,2,1,0:T(1,128)} %copy-done.8) | copy-start | bytes 6148
  205.1 0.6 copy-start.10
  205.7 9.9 %all-to-all-start.10 = ((f32[16,1,1,32]{3,2,1,0:T(1,128)}), f32[16,1,1,32]{3,2,1,0:T(1,128)S(1)}, u32[]{:S(2)}, u32[]{:S(2)}) async-start(f32[16,1,1,32]{3,2,1,0:T(1,128)} %copy.120), calls=%async_computation.10 | async-start | bytes 16384 | tf_op jit(solution)/shard_map/all_to_all | solution.py:112
  215.5 13.5 %all-to-all-start.2 = ((f32[16,1,1,4096]{3,1,2,0:T(1,128)}), f32[16,1,1,4096]{3,1,2,0:T(1,128)S(1)}, u32[]{:S(2)}, u32[]{:S(2)}) async-start(f32[16,1,1,4096]{3,1,2,0:T(1,128)} %bitcast.19), calls=%async_computation.2 | async-start | bytes 524288 | tf_op jit(solution)/shard_map/all_to_all | solution.py:111
  219.1 52.2 %copy-start.1 = (bf16[1920,512]{1,0:T(8,128)(2,1)S(1)}, bf16[1920,512]{1,0:T(8,128)(2,1)}, u32[]{:S(2)}) copy-start(bf16[1920,512]{1,0:T(8,128)(2,1)} %param.16) | copy-start | bytes 5898244
  229.1 13.5 %all-to-all-start.5 = ((f32[16,1,1,4096]{3,1,2,0:T(1,128)}), f32[16,1,1,4096]{3,1,2,0:T(1,128)S(1)}, u32[]{:S(2)}, u32[]{:S(2)}) async-start(f32[16,1,1,4096]{3,1,2,0:T(1,128)} %bitcast.35), calls=%async_computation.5 | async-start | bytes 524288 | tf_op jit(solution)/shard_map/all_to_all | solution.py:111
  242.6 13.5 %all-to-all-start.8 = ((f32[16,1,1,4096]{3,1,2,0:T(1,128)}), f32[16,1,1,4096]{3,1,2,0:T(1,128)S(1)}, u32[]{:S(2)}, u32[]{:S(2)}) async-start(f32[16,1,1,4096]{3,1,2,0:T(1,128)} %bitcast.50), calls=%async_computation.8 | async-start | bytes 524288 | tf_op jit(solution)/shard_map/all_to_all | solution.py:111
  256.2 13.5 %all-to-all-start.11 = ((f32[16,1,1,4096]{3,1,2,0:T(1,128)}), f32[16,1,1,4096]{3,1,2,0:T(1,128)S(1)}, u32[]{:S(2)}, u32[]{:S(2)}) async-start(f32[16,1,1,4096]{3,1,2,0:T(1,128)} %bitcast.65), calls=%async_computation.11 | async-start | bytes 524288 | tf_op jit(solution)/shard_map/all_to_all | solution.py:111
where the time goes:
time: 273 us; the launch traced here: 271 us
  blocking collectives  83.7 us (31%)
  waiting for transfers between devices  59.9 us (22%)
  starting transfers between devices  45.6 us (17%)
  local copies, waits for them, and re-layouts  40.9 us (15%)
  other arithmetic  22.1 us (8%)
  matrix products  17.6 us (6%)
    all_gather x4, blocking collectives, prefix_attention(): whole = lax.all_gather(selected, 'seq', axis=0, tiled=True)  83.7 us
    all_to_all x4, waiting for transfers between devices, prefix_attention(): lax.all_to_all(parts[:, None], 'seq', split_axis=0, concat_axis=1, tiled=...  33.5 us
    all_to_all x4, starting transfers between devices, prefix_attention(): lax.all_to_all(totals[:, None], 'seq', split_axis=0, concat_axis=1, tiled...  17.2 us
    unnamed x61, local copies, waits for them, and re-layouts  14.6 us
    all_to_all x4, starting transfers between devices, prefix_attention(): lax.all_to_all(peaks[:, None], 'seq', split_axis=0, concat_axis=1, tiled=...  14.3 us
    all_to_all x4, starting transfers between devices, prefix_attention(): lax.all_to_all(parts[:, None], 'seq', split_axis=0, concat_axis=1, tiled=...  14.1 us
    another operation x2, local copies, waits for them, and re-layouts  13.9 us
    all_to_all x4, waiting for transfers between devices, prefix_attention(): lax.all_to_all(totals[:, None], 'seq', split_axis=0, concat_axis=1, tiled...  13.8 us
  transfers between devices with their start and end apart: 12, of which 10 were waited for; matrix products, arithmetic and copies ran while one was open for 17% of the time, Pallas kernels for 0%

commit v1 on v0

v1 whole, which is shorter than its diff:
```python
import functools
import math

import jax
import jax.numpy as jnp
import numpy as np
from jax import lax
from jax.experimental import pallas as pl
from jax.experimental.pallas import tpu as pltpu
from jax.sharding import PartitionSpec as P

HD = 128
QH = 32
KVH = 4
BLK = 128
STEPS = 4
SUF = 4096
GROUP = QH // KVH
HALF_KV = KVH // 2
WIDE = HALF_KV * HD
KROWS = GROUP * STEPS
HROWS = HALF_KV * KROWS
ROWS = KVH * KROWS
PAY = HROWS + 16
SCALE = 1.0 / math.sqrt(HD)
EXP2 = SCALE * math.log2(math.e)
LOG2E = math.log2(math.e)
TURN = 2.0 * math.pi / 16777216.0
SUF_TILE = 1024
F32 = jnp.float32
BF16 = jnp.bfloat16


def multipliers():
    half = HD // 2
    index = np.arange(half)
    freq = 500000.0 ** (-2.0 * index / (2 * half))
    return np.floor(2.0**24 * freq / (2 * np.pi)).astype(np.int64)


def phase_rows():
    mult = np.tile(multipliers(), 2)
    table = np.zeros((8, HD), np.int32)
    table[0] = mult >> 12
    table[1] = mult & 4095
    return table


def row_tables():
    mult = np.tile(multipliers(), 2)
    turns = (np.arange(BLK)[:, None] * mult[None, :]) % 16777216
    angle = turns * (2.0 * np.pi / 16777216.0)
    sign = np.where(np.arange(HD) < HD // 2, -1.0, 1.0)
    return (np.cos(angle).astype(np.float32), (np.sin(angle) * sign).astype(np.float32))


def phases(spot, high, low):
    first = spot * low
    second = (spot * high) & 4095
    turns = (first + second * 4096) & 16777215
    return turns.astype(F32) * TURN


def lane_sign(shape):
    lane = lax.broadcasted_iota(jnp.int32, shape, len(shape) - 1)
    return jnp.where(lane < HD // 2, -1.0, 1.0).astype(F32)


def turn(x, cosine, sine):
    return x * cosine + pltpu.roll(x, HD // 2, axis=1) * sine


def query_kernel(prefix, count, len_ref, table_ref, q_ref, nk_ref, send_ref, own_ref, new_ref, rows_ref, nrows_ref):
    step = lax.broadcasted_iota(jnp.int32, (8, HD), 0) % STEPS
    spot = prefix + len_ref[0] + step
    angle = phases(spot, table_ref[0:1, :], table_ref[1:2, :])
    cosine = jnp.cos(angle)
    sine = jnp.sin(angle) * lane_sign((8, HD))
    q = q_ref[0].astype(F32)
    for h in range(QH):
        rows_ref[h * STEPS : (h + 1) * STEPS, :] = q[:, h * HD : (h + 1) * HD]
    for i in range(ROWS // 8):
        rows_ref[i * 8 : i * 8 + 8, :] = turn(rows_ref[i * 8 : i * 8 + 8, :], cosine, sine)
    rotated = rows_ref[...].astype(BF16)
    own_ref[...] = rotated
    for d in range(count):
        part = d % 2
        send_ref[d] = rotated[part * HROWS : (part + 1) * HROWS]
    nrows_ref[...] = jnp.zeros_like(nrows_ref)
    nk = nk_ref[0].astype(F32)
    for k in range(KVH):
        cut = slice(k * HD, (k + 1) * HD)
        nrows_ref[0:STEPS, cut] = turn(nk[:, cut], cosine[0:STEPS], sine[0:STEPS])
    new_ref[...] = nrows_ref[...].astype(BF16)


def rotate_queries(queries, new_keys, suffix_len, prefix, count):
    smem = pl.BlockSpec(memory_space=pltpu.SMEM)
    vmem = pl.BlockSpec(memory_space=pltpu.VMEM)
    return pl.pallas_call(
        functools.partial(query_kernel, prefix, count),
        out_shape=(
            jax.ShapeDtypeStruct((count, HROWS, HD), BF16),
            jax.ShapeDtypeStruct((ROWS, HD), BF16),
            jax.ShapeDtypeStruct((16, KVH * HD), BF16),
        ),
        in_specs=[smem, vmem, vmem, vmem],
        out_specs=(vmem, vmem, vmem),
        scratch_shapes=[pltpu.VMEM((ROWS, HD), F32), pltpu.VMEM((16, KVH * HD), F32)],
        name="rotate_queries",
    )(suffix_len, jnp.asarray(phase_rows()), queries, new_keys)


def project_kernel(
    blocks, core_ref, order_ref, lat_ref, ku_ref, vu_ref, table_ref, rc_ref, rs_ref, k_ref, v_ref, bc_ref, bs_ref
):
    step = pl.program_id(0)

    @pl.when(step == 0)
    def _():
        pad = bc_ref.shape[0]
        row = lax.broadcasted_iota(jnp.int32, (pad, HD), 0)
        spot = jnp.zeros((pad, HD), jnp.int32)
        for b in range(blocks):
            spot = jnp.where(row == b, order_ref[b], spot)
        angle = phases(spot * BLK, table_ref[0:1, :], table_ref[1:2, :])
        bc_ref[...] = jnp.cos(angle)
        bs_ref[...] = jnp.sin(angle) * lane_sign((pad, HD))

    lat = lat_ref[...]
    per = lat.shape[0] // BLK
    keys = jnp.dot(lat, ku_ref[...], preferred_element_type=F32)
    v_ref[...] = jnp.dot(lat, vu_ref[...], preferred_element_type=F32).astype(BF16)
    for i in range(per):
        b = step * per + i
        block_cos = bc_ref[pl.ds(b, 1), :]
        block_sin = bs_ref[pl.ds(b, 1), :]
        cosine = block_cos * rc_ref[...] - block_sin * rs_ref[...]
        sine = block_sin * rc_ref[...] + block_cos * rs_ref[...]
        for k in range(HALF_KV):
            cut = slice(k * HD, (k + 1) * HD)
            part = keys[i * BLK : (i + 1) * BLK, cut]
            k_ref[i * BLK : (i + 1) * BLK, cut] = turn(part, cosine, sine).astype(BF16)


def project(core, order, latent, key_up, value_up):
    pre_rows, rank = latent.shape
    blocks = pre_rows // BLK
    per = max(d for d in range(1, 6) if blocks % d == 0)
    tile = per * BLK
    rc, rs = row_tables()
    fixed = lambda i, c, o: (0, 0)
    half = lambda i, c, o: (0, c[0])
    tiles = lambda i, c, o: (i, 0)
    return pl.pallas_call(
        functools.partial(project_kernel, blocks),
        out_shape=(
            jax.ShapeDtypeStruct((pre_rows, WIDE), BF16),
            jax.ShapeDtypeStruct((pre_rows, WIDE), BF16),
        ),
        grid_spec=pltpu.PrefetchScalarGridSpec(
            num_scalar_prefetch=2,
            grid=(blocks // per,),
            in_specs=[
                pl.BlockSpec((tile, rank), tiles),
                pl.BlockSpec((rank, WIDE), half),
                pl.BlockSpec((rank, WIDE), half),
                pl.BlockSpec((8, HD), fixed),
                pl.BlockSpec((BLK, HD), fixed),
                pl.BlockSpec((BLK, HD), fixed),
            ],
            out_specs=[pl.BlockSpec((tile, WIDE), tiles), pl.BlockSpec((tile, WIDE), tiles)],
            scratch_shapes=[pltpu.VMEM((-(-blocks // 8) * 8, HD), F32)] * 2,
        ),
        cost_estimate=pl.CostEstimate(
            flops=4 * pre_rows * rank * WIDE, bytes_accessed=pre_rows * (rank + 2 * WIDE) * 2, transcendentals=0
        ),
        name="project",
    )(core, order, latent, key_up, value_up, jnp.asarray(phase_rows()), jnp.asarray(rc), jnp.asarray(rs))


def three(x):
    first = x.astype(BF16).astype(F32)
    rest = x - first
    second = rest.astype(BF16).astype(F32)
    return first, second, rest - second


def attend_kernel(q_ref, k0_ref, v0_ref, k1_ref, v1_ref, out_ref):
    reqs = q_ref.shape[0]
    nt = (((1,), (1,)), ((), ()))
    peaks, totals = [], []
    for k in range(HALF_KV):
        cut = slice(k * HD, (k + 1) * HD)
        q = q_ref[:, k * KROWS : (k + 1) * KROWS, :].reshape(reqs * KROWS, HD)
        s0 = lax.dot_general(q, k0_ref[:, cut], nt, preferred_element_type=F32)
        s1 = lax.dot_general(q, k1_ref[:, cut], nt, preferred_element_type=F32)
        peak = jnp.maximum(jnp.max(s0, -1, keepdims=True), jnp.max(s1, -1, keepdims=True))
        e0 = jnp.exp2((s0 - peak) * EXP2)
        e1 = jnp.exp2((s1 - peak) * EXP2)
        total = jnp.sum(e0, -1, keepdims=True) + jnp.sum(e1, -1, keepdims=True)
        o = jnp.dot(e0.astype(BF16), v0_ref[:, cut], preferred_element_type=F32)
        o = o + jnp.dot(e1.astype(BF16), v1_ref[:, cut], preferred_element_type=F32)
        o = o / total
        out_ref[:, k * KROWS : (k + 1) * KROWS, :] = o.astype(BF16).reshape(reqs, KROWS, HD)
        peaks.append(peak * SCALE)
        totals.append(total)
    row = lax.broadcasted_iota(jnp.int32, (KROWS, HD), 0)
    lane = lax.broadcasted_iota(jnp.int32, (KROWS, HD), 1)
    place = lax.broadcasted_iota(jnp.int32, (16, HD), 0)
    for r in range(reqs):
        cut = slice(r * KROWS, (r + 1) * KROWS)
        lines = []
        for parts in (peaks, totals):
            line = jnp.zeros((1, HD), F32)
            for k in range(HALF_KV):
                spread = jnp.where(lane == row + k * KROWS, parts[k][cut], 0.0)
                line = line + jnp.sum(spread, 0, keepdims=True)
            lines.extend(three(line))
        stats = jnp.zeros((16, HD), F32)
        for i, line in enumerate(lines):
            stats = jnp.where(place == i, line, stats)
        out_ref[r, HROWS:PAY, :] = stats.astype(BF16)


def attend(q, k0, v0, k1, v1):
    count = q.shape[0]
    pre_rows = k0.shape[0]
    per = math.gcd(count, 4)
    fixed = lambda i: (0, 0)
    kv = pl.BlockSpec((pre_rows, WIDE), fixed)
    return pl.pallas_call(
        attend_kernel,
        out_shape=jax.ShapeDtypeStruct((count, PAY, HD), BF16),
        grid=(count // per,),
        in_specs=[pl.BlockSpec((per, HROWS, HD), lambda i: (i, 0, 0)), kv, kv, kv, kv],
        out_specs=pl.BlockSpec((per, PAY, HD), lambda i: (i, 0, 0)),
        compiler_params=pltpu.CompilerParams(vmem_limit_bytes=40 << 20),
        cost_estimate=pl.CostEstimate(
            flops=8 * count * HROWS * HD * pre_rows,
            bytes_accessed=8 * pre_rows * WIDE,
            transcendentals=2 * count * HROWS * pre_rows,
        ),
        name="attend",
    )(q, k0, v0, k1, v1)


def suffix_kernel(len_ref, q_ref, nk_ref, nv_ref, k_ref, v_ref, acc_ref, peak_ref, total_ref):
    step = pl.program_id(0)
    length = len_ref[0]
    tile = k_ref.shape[1]
    nt = (((1,), (1,)), ((), ()))

    def scores(keys):
        return jnp.concatenate(
            [
                lax.dot_general(
                    q_ref[k * KROWS : (k + 1) * KROWS, :],
                    keys[:, k * HD : (k + 1) * HD],
                    nt,
                    preferred_element_type=F32,
                )
                for k in range(KVH)
            ],
            0,
        )

    def weigh(probs, values):
        probs = probs.astype(BF16)
        return jnp.concatenate(
            [
                jnp.dot(
                    probs[k * KROWS : (k + 1) * KROWS],
                    values[:, k * HD : (k + 1) * HD],
                    preferred_element_type=F32,
                )
                for k in range(KVH)
            ],
            0,
        )

    @pl.when(step == 0)
    def _():
        s = scores(nk_ref[...])
        row = lax.broadcasted_iota(jnp.int32, s.shape, 0) % STEPS
        lane = lax.broadcasted_iota(jnp.int32, s.shape, 1)
        s = jnp.where(lane <= row, s, -jnp.inf)
        peak = jnp.max(s, -1, keepdims=True)
        e = jnp.exp2((s - peak) * EXP2)
        acc_ref[...] = weigh(e, nv_ref[...])
        peak_ref[...] = jnp.broadcast_to(peak, peak_ref.shape)
        total_ref[...] = jnp.broadcast_to(jnp.sum(e, -1, keepdims=True), total_ref.shape)

    @pl.when(step * tile < length)
    def _():
        s = scores(k_ref[0])
        spot = step * tile + lax.broadcasted_iota(jnp.int32, s.shape, 1)
        s = jnp.where(spot < length, s, -jnp.inf)
        old = peak_ref[:, 0:1]
        peak = jnp.maximum(old, jnp.max(s, -1, keepdims=True))
        keep = jnp.exp2((old - peak) * EXP2)
        e = jnp.exp2((s - peak) * EXP2)
        acc_ref[...] = acc_ref[...] * keep + weigh(e, v_ref[0])
        total_ref[...] = total_ref[...] * keep + jnp.sum(e, -1, keepdims=True)
        peak_ref[...] = jnp.broadcast_to(peak, peak_ref.shape)

    @pl.when(step == pl.num_programs(0) - 1)
    def _():
        peak_ref[...] = peak_ref[...] * SCALE


def suffix(length, q, new_rot, new_values, keys, values):
    tile = SUF_TILE
    fixed = lambda i, n: (0, 0)
    walk = lambda i, n: (0, jnp.minimum(i, (n[0] - 1) // tile), 0)
    out = jax.ShapeDtypeStruct((ROWS, HD), F32)
    return pl.pallas_call(
        suffix_kernel,
        out_shape=(out, out, out),
        grid_spec=pltpu.PrefetchScalarGridSpec(
            num_scalar_prefetch=1,
            grid=(SUF // tile,),
            in_specs=[
                pl.BlockSpec((ROWS, HD), fixed),
                pl.BlockSpec((16, KVH * HD), fixed),
                pl.BlockSpec((16, KVH * HD), fixed),
                pl.BlockSpec((1, tile, KVH * HD), walk),
                pl.BlockSpec((1, tile, KVH * HD), walk),
            ],
            out_specs=[pl.BlockSpec((ROWS, HD), fixed)] * 3,
        ),
        cost_estimate=pl.CostEstimate(
            flops=4 * ROWS * SUF * HD, bytes_accessed=4 * SUF * KVH * HD, transcendentals=ROWS * SUF
        ),
        name="suffix",
    )(length, q, new_rot, new_values, keys, values)


def combine_kernel(got_ref, acc_ref, peak_ref, total_ref, out_ref):
    count = got_ref.shape[0]
    row = lax.broadcasted_iota(jnp.int32, (HROWS, HD), 0)
    lane = lax.broadcasted_iota(jnp.int32, (HROWS, HD), 1)
    eye = row == lane

    def column(line):
        return jnp.sum(jnp.where(eye, line, 0.0), -1, keepdims=True)

    for part in range(2):
        sources = range(part, count, 2)
        stats = [got_ref[j, HROWS:PAY, :].astype(F32) for j in sources]
        peaks = [s[0:1] + s[1:2] + s[2:3] for s in stats]
        totals = [s[3:4] + s[4:5] + s[5:6] for s in stats]
        top = functools.reduce(jnp.maximum, peaks)
        factors = [t * jnp.exp2((p - top) * LOG2E) for p, t in zip(peaks, totals)]
        denom = column(sum(factors))
        top = column(top)
        numer = jnp.zeros((HROWS, HD), F32)
        for j, factor in zip(sources, factors):
            numer = numer + column(factor) * got_ref[j, 0:HROWS, :].astype(F32)
        cut = slice(part * HROWS, (part + 1) * HROWS)
        near = peak_ref[cut, :]
        big = jnp.maximum(top, near)
        far_weight = jnp.exp2((top - big) * LOG2E)
        near_weight = jnp.exp2((near - big) * LOG2E)
        result = (numer * far_weight + acc_ref[cut, :] * near_weight) / (
            denom * far_weight + total_ref[cut, :] * near_weight
        )
        for h in range(HROWS // STEPS):
            at = part * (HROWS // STEPS) + h
            out_ref[0, :, at * HD : (at + 1) * HD] = result[h * STEPS : (h + 1) * STEPS].astype(BF16)


def combine(got, acc, peak, total):
    vmem = pl.BlockSpec(memory_space=pltpu.VMEM)
    return pl.pallas_call(
        combine_kernel,
        out_shape=jax.ShapeDtypeStruct((1, STEPS, QH * HD), BF16),
        in_specs=[vmem] * 4,
        out_specs=vmem,
        name="combine",
    )(got, acc, peak, total)


def local(
    prefix_latent,
    block_order,
    key_up,
    value_up,
    queries,
    new_keys,
    new_values,
    suffix_keys,
    suffix_values,
    suffix_len,
):
    count = lax.axis_size("seq")
    prefix = prefix_latent.shape[0] * count
    core = (lax.axis_index("seq") % 2).astype(jnp.int32)[None]
    swap = [(i, i ^ 1) for i in range(count)]
    send, own, new_rot = rotate_queries(queries, new_keys, suffix_len, prefix, count)
    other_latent = lax.ppermute(prefix_latent, "seq", swap)
    other_order = lax.ppermute(block_order, "seq", swap)
    gathered = lax.all_to_all(send, "seq", split_axis=0, concat_axis=0, tiled=True)
    k0, v0 = project(core, block_order, prefix_latent, key_up, value_up)
    k1, v1 = project(core, other_order, other_latent, key_up, value_up)
    parts = attend(gathered, k0, v0, k1, v1)
    got = lax.all_to_all(parts, "seq", split_axis=0, concat_axis=0, tiled=True)
    new_pad = jnp.pad(new_values[0], ((0, 16 - STEPS), (0, 0)))
    acc, peak, total = suffix(suffix_len, own, new_rot, new_pad, suffix_keys, suffix_values)
    return combine(got, acc, peak, total)


def solution(mesh):
    placed = (
        P(("parts", "seq"), None),
        P(("parts", "seq")),
        P(),
        P(),
        P(("parts", "seq"), None, None),
        P(("parts", "seq"), None, None),
        P(("parts", "seq"), None, None),
        P(("parts", "seq"), None, None),
        P(("parts", "seq"), None, None),
        P(("parts", "seq")),
    )
    return jax.shard_map(
        local,
        mesh=mesh,
        in_specs=placed,
        out_specs=P(("parts", "seq"), None, None),
        check_vma=False,
    )
```

time: 273 us -> 55.8 us (0.20)
  blocking collectives: 83.7 us -> 0 us
  waiting for transfers between devices: 59.9 us -> 6.92 us
  local copies, waits for them, and re-layouts: 40.9 us -> 7.99 us
  starting transfers between devices: 45.6 us -> 13.7 us
  Pallas kernels: 0 us -> 25.8 us
  other arithmetic: 22.1 us -> 0 us
  matrix products: 17.6 us -> 0 us
    all_gather x4 -> x0, blocking collectives: 83.7 us -> none  [prefix_attention(): whole = lax.all_gather(selected, 'seq', axis=0, tiled=True)]
    all_to_all x12 -> x2, waiting for transfers between devices: 59.9 us -> 6.92 us  [the longest x1 6.91 us: local(): got = lax.all_to_all(parts, 'seq', split_axis=0, concat_axis=0, tiled=True)]
    all_to_all x12 -> x2, starting transfers between devices: 45.6 us -> 12.8 us  [the longest x1 7.05 us: local(): lax.all_to_all(send, 'seq', split_axis=0, concat_axis=0, tiled=True)]
    pallas_call x0 -> x6, Pallas kernels: none -> 25.8 us  [the longest x2 10.4 us: project(): pl.pallas_call(functools.partial(project_kernel, blocks), out_shape=(jax....]
    another operation x10 -> x0, local copies, waits for them, and re-layouts: 19.2 us -> none
    dot_general x14 -> x0, matrix products: 17.6 us -> none  [the longest x1 3.82 us: local(): jnp.einsum('rtkgd,rpkd->rtkgp', split, cache_keys, preferred_element_type...]
    unnamed x61 -> x16, local copies, waits for them, and re-layouts: 14.6 us -> 7.39 us
    reduce_sum x14 -> x0, other arithmetic: 5.61 us -> none  [the longest x4 3.1 us: shard_part(): total = jnp.sum(expo, -1)]
  transfers between devices with their start and end apart: 12 -> 4, of which waited for: 10 -> 1; matrix products, arithmetic and copies ran while one was open for 17% -> 1% of each run, Pallas kernels for 0% -> 28%
where the time goes in v1:
time: 55.8 us; the launch traced here: 55.1 us
  Pallas kernels  25.8 us (46%)
  starting transfers between devices  13.7 us (25%)
  local copies, waits for them, and re-layouts  7.99 us (14%)
  waiting for transfers between devices  6.92 us (12%)
  between operations  0.72 us (1%)
    pallas_call x2, Pallas kernels, project(): pl.pallas_call(functools.partial(project_kernel, blocks), out_shape=(jax....  10.4 us
    pallas_call x1, Pallas kernels, attend(): pl.pallas_call(attend_kernel, out_shape=jax.ShapeDtypeStruct((count, PAY,...  8.34 us
    unnamed x16, local copies, waits for them, and re-layouts  7.39 us
    all_to_all x1, starting transfers between devices, local(): lax.all_to_all(send, 'seq', split_axis=0, concat_axis=0, tiled=True)  7.05 us
    all_to_all x1, waiting for transfers between devices, local(): got = lax.all_to_all(parts, 'seq', split_axis=0, concat_axis=0, tiled=True)  6.91 us
    all_to_all x1, starting transfers between devices, local(): got = lax.all_to_all(parts, 'seq', split_axis=0, concat_axis=0, tiled=True)  5.77 us
    pallas_call x1, Pallas kernels, suffix(): pl.pallas_call(suffix_kernel, out_shape=(out, out, out), grid_spec=pltpu....  3.57 us
    pallas_call x1, Pallas kernels, combine(): pl.pallas_call(combine_kernel, out_shape=jax.ShapeDtypeStruct((1, STEPS,...  1.9 us
  transfers between devices with their start and end apart: 4, of which 1 were waited for; matrix products, arithmetic and copies ran while one was open for 1% of the time, Pallas kernels for 28%

profile of v1, /device:TPU:0, one launch (start us, length us, event | category | flops | bytes accessed | tf_op | source)
XLA Modules:
  0.0 55.1 jit_solution(12134209112344627396)
XLA Ops:
  0.0 0.5 collective-permute-start.1
  1.1 1.6 %rotate_queries.1 = (bf16[16,64,128]{2,1,0:T(8,128)(2,1)}, bf16[128,128]{1,0:T(8,128)(2,1)}, bf16[16,512]{1,0:T(8,128)(2,1)}) custom-call(s32[1]{0:T(128)S(6)} %copy.18.len_ref, s32[8,128]{1,0:T(8,128)} %constant.26.clone.table_ref, bf16[1,4,4096]{2,1,0:T(4,128)(2,1)} %q_ref.1, bf16[1,4,512]{2,1,0:T(4,128)(2,1)} %nk_ref.1), custom_call_target="tpu_custom_call" | custom-call | tf_op jit(solution)/shard_map/rotate_queries/pallas_call | solution.py:100
  2.7 7.0 %all-to-all-start = ((bf16[16,64,128]{2,1,0:T(8,128)(2,1)}), bf16[16,64,128]{2,1,0:T(8,128)(2,1)S(1)}, u32[]{:S(2)}, u32[]{:S(2)}) async-start(bf16[16,64,128]{2,1,0:T(8,128)(2,1)} %get-tuple-element.15), calls=%async_computation | async-start | bytes 524288 | tf_op jit(solution)/shard_map/all_to_all | solution.py:403
  9.7 0.4 collective-permute-start
  10.1 5.2 %project.2 = (bf16[1920,256]{1,0:T(8,128)(2,1)}, bf16[1920,256]{1,0:T(8,128)(2,1)}) custom-call(s32[1]{0:T(128)} %bitcast.core_ref, s32[15]{0:T(128)} %order_ref.1, bf16[1920,512]{1,0:T(8,128)(2,1)} %lat_ref.1, bf16[512,512]{1,0:T(8,128)(2,1)} %ku_ref.3, bf16[512,512]{1,0:T(8,128)(2,1)} %vu_ref.3, s32[8,128]{1,0:T(8,128)} %constant.26.clone.table_ref, ...), custom_call_target="tpu_custom_call" | custom-call | flops 1006632960 | bytes 3932160 | tf_op jit(solution)/shard_map/project/pallas_call | solution.py:155
  15.4 0.0 collective-permute-done.order_ref
  15.4 0.0 copy-start.7
  15.4 0.0 collective-permute-done.1.lat_ref
  15.4 0.6 %copy-done.7 = s32[15]{0:T(128)} copy-done((s32[15]{0:T(128)}, s32[15]{0:T(128)S(1)}, u32[]{:S(2)}) %copy-start.7) | copy-done | bytes 84
  15.9 0.0 copy-start.6
  15.9 1.3 %copy-done.6 = bf16[1920,512]{1,0:T(8,128)(2,1)} copy-done((bf16[1920,512]{1,0:T(8,128)(2,1)}, bf16[1920,512]{1,0:T(8,128)(2,1)S(1)}, u32[]{:S(2)}) %copy-start.6) | copy-done | bytes 1966104
  17.2 5.2 %project.3 = (bf16[1920,256]{1,0:T(8,128)(2,1)}, bf16[1920,256]{1,0:T(8,128)(2,1)}) custom-call(s32[1]{0:T(128)} %bitcast.core_ref, s32[15]{0:T(128)} %copy-done.7, bf16[1920,512]{1,0:T(8,128)(2,1)} %copy-done.6, bf16[512,512]{1,0:T(8,128)(2,1)} %ku_ref.3, bf16[512,512]{1,0:T(8,128)(2,1)} %vu_ref.3, s32[8,128]{1,0:T(8,128)} %constant.26.clone.table_ref, ...), custom_call_target="tpu_custom_call" | custom-call | flops 1006632960 | bytes 3932160 | tf_op jit(solution)/shard_map/project/pallas_call | solution.py:155
  22.5 0.0 copy-start.5
  22.5 0.0 all-to-all-done.q_ref
  22.5 0.0 copy-start
  22.5 1.2 %copy-done = bf16[1920,256]{1,0:T(8,128)(2,1)S(1)} copy-done((bf16[1920,256]{1,0:T(8,128)(2,1)S(1)}, bf16[1920,256]{1,0:T(8,128)(2,1)}, u32[]{:S(2)}) %copy-start) | copy-done | bytes 983064
  23.7 0.0 copy-start.1
  23.7 1.2 %copy-done.1 = bf16[1920,256]{1,0:T(8,128)(2,1)S(1)} copy-done((bf16[1920,256]{1,0:T(8,128)(2,1)S(1)}, bf16[1920,256]{1,0:T(8,128)(2,1)}, u32[]{:S(2)}) %copy-start.1) | copy-done | bytes 983064
  24.9 0.0 copy-start.2
  24.9 1.2 %copy-done.2 = bf16[1920,256]{1,0:T(8,128)(2,1)S(1)} copy-done((bf16[1920,256]{1,0:T(8,128)(2,1)S(1)}, bf16[1920,256]{1,0:T(8,128)(2,1)}, u32[]{:S(2)}) %copy-start.2) | copy-done | bytes 983064
  26.1 0.0 copy-start.3
  26.1 1.2 %copy-done.3 = bf16[1920,256]{1,0:T(8,128)(2,1)S(1)} copy-done((bf16[1920,256]{1,0:T(8,128)(2,1)S(1)}, bf16[1920,256]{1,0:T(8,128)(2,1)}, u32[]{:S(2)}) %copy-start.3) | copy-done | bytes 983064
  27.3 8.3 %attend.1 = bf16[16,80,128]{2,1,0:T(8,128)(2,1)} custom-call(bf16[16,64,128]{2,1,0:T(8,128)(2,1)S(1)} %all-to-all-done.q_ref, bf16[1920,256]{1,0:T(8,128)(2,1)S(1)} %copy-done, bf16[1920,256]{1,0:T(8,128)(2,1)S(1)} %copy-done.1, bf16[1920,256]{1,0:T(8,128)(2,1)S(1)} %copy-done.2, bf16[1920,256]{1,0:T(8,128)(2,1)S(1)} %copy-done.3), custom_call_target="tpu_custom_call" | custom-call | flops 2013265920 | bytes 3932160 | tf_op jit(solution)/shard_map/attend/pallas_call | solution.py:232
  35.6 5.8 %all-to-all-start.1 = ((bf16[16,80,128]{2,1,0:T(8,128)(2,1)}), bf16[16,80,128]{2,1,0:T(8,128)(2,1)S(1)}, u32[]{:S(2)}, u32[]{:S(2)}) async-start(bf16[16,80,128]{2,1,0:T(8,128)(2,1)} %attend.1), calls=%async_computation.1 | async-start | bytes 655360 | tf_op jit(solution)/shard_map/all_to_all | solution.py:407
  41.4 0.0 copy-done.5
  41.4 0.6 %pad.4.nv_ref = bf16[16,512]{1,0:T(8,128)(2,1)} pad(bf16[4,512]{1,0:T(4,128)(2,1)S(1)} %bitcast.2, bf16[]{:T(256)} %constant.25.clone.1), padding=0_12x0_0 | pad | bytes 20482 | tf_op jit(solution)/shard_map/jit(_pad)/pad | solution.py:408
  42.0 3.6 %suffix.1 = (f32[128,128]{1,0:T(8,128)}, f32[128,128]{1,0:T(8,128)}, f32[128,128]{1,0:T(8,128)}) custom-call(s32[1]{0:T(128)S(6)} %copy.18.len_ref, bf16[128,128]{1,0:T(8,128)(2,1)} %get-tuple-element.20.q_ref, bf16[16,512]{1,0:T(8,128)(2,1)} %get-tuple-element.21.nk_ref, bf16[16,512]{1,0:T(8,128)(2,1)} %pad.4.nv_ref, bf16[1,4096,512]{2,1,0:T(8,128)(2,1)} %k_ref.1, ...), custom_call_target="tpu_custom_call" | custom-call | flops 268435456 | bytes 8388608 | tf_op jit(solution)/shard_map/suffix/pallas_call | solution.py:317
  45.6 6.9 %all-to-all-done.1.got_ref = bf16[16,80,128]{2,1,0:T(8,128)(2,1)S(1)} async-done(((bf16[16,80,128]{2,1,0:T(8,128)(2,1)}), bf16[16,80,128]{2,1,0:T(8,128)(2,1)S(1)}, u32[]{:S(2)}, u32[]{:S(2)}) %all-to-all-start.1) | async-done | bytes 327712 | tf_op jit(solution)/shard_map/all_to_all | solution.py:407
  52.5 0.0 copy-start.4
  52.5 0.7 %copy-done.4 = bf16[16,80,128]{2,1,0:T(8,128)(2,1)} copy-done((bf16[16,80,128]{2,1,0:T(8,128)(2,1)}, bf16[16,80,128]{2,1,0:T(8,128)(2,1)S(1)}, u32[]{:S(2)}) %copy-start.4) | copy-done | bytes 327704
  53.2 1.9 %combine.1 = bf16[1,4,4096]{2,1,0:T(4,128)(2,1)} custom-call(bf16[16,80,128]{2,1,0:T(8,128)(2,1)} %copy-done.4, f32[128,128]{1,0:T(8,128)} %get-tuple-element.22.acc_ref, f32[128,128]{1,0:T(8,128)} %get-tuple-element.23.peak_ref, f32[128,128]{1,0:T(8,128)} %get-tuple-element.24.total_ref), custom_call_target="tpu_custom_call" | custom-call | tf_op jit(solution)/shard_map/combine/pallas_call | solution.py:375
Async XLA Ops:
  0.0 15.4 %collective-permute-start.1 = (bf16[1920,512]{1,0:T(8,128)(2,1)}, bf16[1920,512]{1,0:T(8,128)(2,1)S(1)}, u32[]{:S(2)}, u32[]{:S(2)}) collective-permute-start(bf16[1920,512]{1,0:T(8,128)(2,1)} %lat_ref.1), channel_id=1, source_target_pairs={{0,1},{1,0},{2,3},{3,2},{4,5},{5,4},{6,7},{7,6},{8,9},{9,8},{10,11... | collective-permute-start | bytes 5898248 | tf_op jit(solution)/shard_map/ppermute | solution.py:401
  2.7 19.8 %all-to-all-start = ((bf16[16,64,128]{2,1,0:T(8,128)(2,1)}), bf16[16,64,128]{2,1,0:T(8,128)(2,1)S(1)}, u32[]{:S(2)}, u32[]{:S(2)}) async-start(bf16[16,64,128]{2,1,0:T(8,128)(2,1)} %get-tuple-element.15), calls=%async_computation | async-start | bytes 524288 | tf_op jit(solution)/shard_map/all_to_all | solution.py:403
  9.7 5.6 %collective-permute-start = (s32[15]{0:T(128)}, s32[15]{0:T(128)S(1)}, u32[]{:S(2)}, u32[]{:S(2)}) collective-permute-start(s32[15]{0:T(128)} %order_ref.1), channel_id=1, source_target_pairs={{0,1},{1,0},{2,3},{3,2},{4,5},{5,4},{6,7},{7,6},{8,9},{9,8},{10,11... | collective-permute-start | bytes 188 | tf_op jit(solution)/shard_map/ppermute | solution.py:402
  15.4 0.6 %copy-start.7 = (s32[15]{0:T(128)}, s32[15]{0:T(128)S(1)}, u32[]{:S(2)}) copy-start(s32[15]{0:T(128)S(1)} %collective-permute-done.order_ref) | copy-start | bytes 184
  15.9 1.3 %copy-start.6 = (bf16[1920,512]{1,0:T(8,128)(2,1)}, bf16[1920,512]{1,0:T(8,128)(2,1)S(1)}, u32[]{:S(2)}) copy-start(bf16[1920,512]{1,0:T(8,128)(2,1)S(1)} %collective-permute-done.1.lat_ref) | copy-start | bytes 5898244
  22.5 18.9 %copy-start.5 = (bf16[1,4,512]{2,1,0:T(4,128)(2,1)S(1)}, bf16[1,4,512]{2,1,0:T(4,128)(2,1)}, u32[]{:S(2)}) copy-start(bf16[1,4,512]{2,1,0:T(4,128)(2,1)} %param.23) | copy-start | bytes 12292
  22.5 1.2 %copy-start = (bf16[1920,256]{1,0:T(8,128)(2,1)S(1)}, bf16[1920,256]{1,0:T(8,128)(2,1)}, u32[]{:S(2)}) copy-start(bf16[1920,256]{1,0:T(8,128)(2,1)} %get-tuple-element.16.k0_ref) | copy-start | bytes 2949124
  23.7 1.2 %copy-start.1 = (bf16[1920,256]{1,0:T(8,128)(2,1)S(1)}, bf16[1920,256]{1,0:T(8,128)(2,1)}, u32[]{:S(2)}) copy-start(bf16[1920,256]{1,0:T(8,128)(2,1)} %get-tuple-element.17.v0_ref) | copy-start | bytes 2949124
  24.9 1.2 %copy-start.2 = (bf16[1920,256]{1,0:T(8,128)(2,1)S(1)}, bf16[1920,256]{1,0:T(8,128)(2,1)}, u32[]{:S(2)}) copy-start(bf16[1920,256]{1,0:T(8,128)(2,1)} %get-tuple-element.18.k1_ref) | copy-start | bytes 2949124
  26.1 1.2 %copy-start.3 = (bf16[1920,256]{1,0:T(8,128)(2,1)S(1)}, bf16[1920,256]{1,0:T(8,128)(2,1)}, u32[]{:S(2)}) copy-start(bf16[1920,256]{1,0:T(8,128)(2,1)} %get-tuple-element.19.v1_ref) | copy-start | bytes 2949124
  35.6 16.9 %all-to-all-start.1 = ((bf16[16,80,128]{2,1,0:T(8,128)(2,1)}), bf16[16,80,128]{2,1,0:T(8,128)(2,1)S(1)}, u32[]{:S(2)}, u32[]{:S(2)}) async-start(bf16[16,80,128]{2,1,0:T(8,128)(2,1)} %attend.1), calls=%async_computation.1 | async-start | bytes 655360 | tf_op jit(solution)/shard_map/all_to_all | solution.py:407
  52.5 0.7 %copy-start.4 = (bf16[16,80,128]{2,1,0:T(8,128)(2,1)}, bf16[16,80,128]{2,1,0:T(8,128)(2,1)S(1)}, u32[]{:S(2)}) copy-start(bf16[16,80,128]{2,1,0:T(8,128)(2,1)S(1)} %all-to-all-done.1.got_ref) | copy-start | bytes 983044

commit v2 on v1

--- a/solution.py
+++ b/solution.py
@@ -21,12 +21,15 @@
 KROWS = GROUP * STEPS
 HROWS = HALF_KV * KROWS
 ROWS = KVH * KROWS
-PAY = HROWS + 16
+PAY = HROWS + 8
 SCALE = 1.0 / math.sqrt(HD)
 EXP2 = SCALE * math.log2(math.e)
 LOG2E = math.log2(math.e)
 TURN = 2.0 * math.pi / 16777216.0
 SUF_TILE = 1024
+PER = 5
+Q_GROUP = 16
+CHUNKS = 5
 F32 = jnp.float32
 BF16 = jnp.bfloat16
 
@@ -112,71 +115,128 @@
 
 
 def project_kernel(
-    blocks, core_ref, order_ref, lat_ref, ku_ref, vu_ref, table_ref, rc_ref, rs_ref, k_ref, v_ref, bc_ref, bs_ref
+    core_ref,
+    order0_ref,
+    order1_ref,
+    lat0_hbm,
+    lat1_hbm,
+    ku_hbm,
+    vu_hbm,
+    table_ref,
+    rc_ref,
+    rs_ref,
+    k_hbm,
+    v_hbm,
+    bc_ref,
+    bs_ref,
+    lat_ref,
+    ku_ref,
+    vu_ref,
+    k_ref,
+    v_ref,
+    in_sem,
+    w_sem,
+    out_sem,
 ):
-    step = pl.program_id(0)
-
-    @pl.when(step == 0)
-    def _():
-        pad = bc_ref.shape[0]
-        row = lax.broadcasted_iota(jnp.int32, (pad, HD), 0)
-        spot = jnp.zeros((pad, HD), jnp.int32)
+    pre_rows = lat0_hbm.shape[0]
+    blocks = pre_rows // BLK
+    per = max(d for d in range(1, PER + 1) if blocks % d == 0)
+    chunks = blocks // per
+    size = per * BLK
+    mine = pl.ds(pl.multiple_of(core_ref[0] * WIDE, WIDE), WIDE)
+    loads = [
+        pltpu.make_async_copy(ku_hbm.at[:, mine], ku_ref, w_sem.at[0]),
+        pltpu.make_async_copy(vu_hbm.at[:, mine], vu_ref, w_sem.at[1]),
+    ]
+    fetches = []
+    for side, source in enumerate((lat0_hbm, lat1_hbm)):
+        for c in range(chunks):
+            at = pl.ds(c * size, size)
+            slot = side * chunks + c
+            fetches.append(pltpu.make_async_copy(source.at[at], lat_ref.at[pl.ds(slot * size, size)], in_sem.at[slot]))
+    loads[0].start()
+    fetches[0].start()
+    loads[1].start()
+    for fetch in fetches[1:]:
+        fetch.start()
+    pad = bc_ref.shape[0]
+    row = lax.broadcasted_iota(jnp.int32, (pad, HD), 0)
+    spot = jnp.zeros((pad, HD), jnp.int32)
+    for side, order_ref in enumerate((order0_ref, order1_ref)):
         for b in range(blocks):
-            spot = jnp.where(row == b, order_ref[b], spot)
-        angle = phases(spot * BLK, table_ref[0:1, :], table_ref[1:2, :])
-        bc_ref[...] = jnp.cos(angle)
-        bs_ref[...] = jnp.sin(angle) * lane_sign((pad, HD))
-
-    lat = lat_ref[...]
-    per = lat.shape[0] // BLK
-    keys = jnp.dot(lat, ku_ref[...], preferred_element_type=F32)
-    v_ref[...] = jnp.dot(lat, vu_ref[...], preferred_element_type=F32).astype(BF16)
-    for i in range(per):
-        b = step * per + i
-        block_cos = bc_ref[pl.ds(b, 1), :]
-        block_sin = bs_ref[pl.ds(b, 1), :]
-        cosine = block_cos * rc_ref[...] - block_sin * rs_ref[...]
-        sine = block_sin * rc_ref[...] + block_cos * rs_ref[...]
+            spot = jnp.where(row == side * blocks + b, order_ref[b], spot)
+    angle = phases(spot * BLK, table_ref[0:1, :], table_ref[1:2, :])
+    bc_ref[...] = jnp.cos(angle)
+    bs_ref[...] = jnp.sin(angle) * lane_sign((pad, HD))
+    loads[0].wait()
+    loads[1].wait()
+    stores = []
+    for slot in range(2 * chunks):
+        at = pl.ds(slot * size, size)
+        fetches[slot].wait()
+        lat = lat_ref[at, :]
+        keys = jnp.dot(lat, ku_ref[...], preferred_element_type=F32)
+        values = jnp.dot(lat, vu_ref[...], preferred_element_type=F32).astype(BF16)
         for k in range(HALF_KV):
-            cut = slice(k * HD, (k + 1) * HD)
-            part = keys[i * BLK : (i + 1) * BLK, cut]
-            k_ref[i * BLK : (i + 1) * BLK, cut] = turn(part, cosine, sine).astype(BF16)
-
-
-def project(core, order, latent, key_up, value_up):
-    pre_rows, rank = latent.shape
+            v_ref[k, at, :] = values[:, k * HD : (k + 1) * HD]
+        for i in range(per):
+            b = slot * per + i
+            block_cos = bc_ref[b : b + 1, :]
+            block_sin = bs_ref[b : b + 1, :]
+            cosine = block_cos * rc_ref[...] - block_sin * rs_ref[...]
+            sine = block_sin * rc_ref[...] + block_cos * rs_ref[...]
+            for k in range(HALF_KV):
+                part = keys[i * BLK : (i + 1) * BLK, k * HD : (k + 1) * HD]
+                k_ref[k, b * BLK : (b + 1) * BLK, :] = turn(part, cosine, sine).astype(BF16)
+        for k in range(HALF_KV):
+            for kind, (source, target) in enumerate(((k_ref, k_hbm), (v_ref, v_hbm))):
+                sem = out_sem.at[(slot * HALF_KV + k) * 2 + kind]
+                store = pltpu.make_async_copy(source.at[k, at], target.at[k, at], sem)
+                store.start()
+                stores.append(store)
+    for store in stores:
+        store.wait()
+
+
+def project(core, order0, order1, latent0, latent1, key_up, value_up):
+    pre_rows, rank = latent0.shape
     blocks = pre_rows // BLK
-    per = max(d for d in range(1, 6) if blocks % d == 0)
-    tile = per * BLK
+    per = max(d for d in range(1, PER + 1) if blocks % d == 0)
+    slots = 2 * blocks // per
+    rows = 2 * pre_rows
     rc, rs = row_tables()
-    fixed = lambda i, c, o: (0, 0)
-    half = lambda i, c, o: (0, c[0])
-    tiles = lambda i, c, o: (i, 0)
+    smem = pl.BlockSpec(memory_space=pltpu.SMEM)
+    vmem = pl.BlockSpec(memory_space=pltpu.VMEM)
+    hbm = pl.BlockSpec(memory_space=pl.ANY)
+    pad = -(-2 * blocks // 8) * 8
+    out = jax.ShapeDtypeStruct((HALF_KV, rows, HD), BF16)
     return pl.pallas_call(
-        functools.partial(project_kernel, blocks),
-        out_shape=(
-            jax.ShapeDtypeStruct((pre_rows, WIDE), BF16),
-            jax.ShapeDtypeStruct((pre_rows, WIDE), BF16),
+        project_kernel,
+        out_shape=(out, out),
+        in_specs=[smem, smem, smem, hbm, hbm, hbm, hbm, vmem, vmem, vmem],
+        out_specs=(hbm, hbm),
+        scratch_shapes=[
+            pltpu.VMEM((pad, HD), F32),
+            pltpu.VMEM((pad, HD), F32),
+            pltpu.VMEM((rows, rank), BF16),
+            pltpu.VMEM((rank, WIDE), BF16),
+            pltpu.VMEM((rank, WIDE), BF16),
+            pltpu.VMEM((HALF_KV, rows, HD), BF16),
+            pltpu.VMEM((HALF_KV, rows, HD), BF16),
+            pltpu.SemaphoreType.DMA((slots,)),
+            pltpu.SemaphoreType.DMA((2,)),
+            pltpu.SemaphoreType.DMA((slots * HALF_KV * 2,)),
+        ],
+        cost_estimate=pl.CostEstimate(
+            flops=4 * rows * rank * WIDE, bytes_accessed=rows * (rank + 2 * WIDE) * 2, transcendentals=0
         ),
-        grid_spec=pltpu.PrefetchScalarGridSpec(
-            num_scalar_prefetch=2,
-            grid=(blocks // per,),
-            in_specs=[
-                pl.BlockSpec((tile, rank), tiles),
-                pl.BlockSpec((rank, WIDE), half),
-                pl.BlockSpec((rank, WIDE), half),
-                pl.BlockSpec((8, HD), fixed),
-                pl.BlockSpec((BLK, HD), fixed),
-                pl.BlockSpec((BLK, HD), fixed),
-            ],
-            out_specs=[pl.BlockSpec((tile, WIDE), tiles), pl.BlockSpec((tile, WIDE), tiles)],
-            scratch_shapes=[pltpu.VMEM((-(-blocks // 8) * 8, HD), F32)] * 2,
-        ),
-        cost_estimate=pl.CostEstimate(
-            flops=4 * pre_rows * rank * WIDE, bytes_accessed=pre_rows * (rank + 2 * WIDE) * 2, transcendentals=0
-        ),
+        compiler_params=pltpu.CompilerParams(vmem_limit_bytes=(64 << 20) - 2200000),
         name="project",
-    )(core, order, latent, key_up, value_up, jnp.asarray(phase_rows()), jnp.asarray(rc), jnp.asarray(rs))
+    )(core, order0, order1, far(latent0), latent1, far(key_up), far(value_up), jnp.asarray(phase_rows()), jnp.asarray(rc), jnp.asarray(rs))
+
+
+def far(x):
+    return pltpu.with_memory_space_constraint(x, pltpu.HBM)
 
 
 def three(x):
@@ -186,63 +246,92 @@
     return first, second, rest - second
 
 
-def attend_kernel(q_ref, k0_ref, v0_ref, k1_ref, v1_ref, out_ref):
-    reqs = q_ref.shape[0]
+def attend_kernel(per, q_ref, k_hbm, v_hbm, out_ref, k_ref, v_ref, stat_ref, sem):
     nt = (((1,), (1,)), ((), ()))
-    peaks, totals = [], []
-    for k in range(HALF_KV):
-        cut = slice(k * HD, (k + 1) * HD)
-        q = q_ref[:, k * KROWS : (k + 1) * KROWS, :].reshape(reqs * KROWS, HD)
-        s0 = lax.dot_general(q, k0_ref[:, cut], nt, preferred_element_type=F32)
-        s1 = lax.dot_general(q, k1_ref[:, cut], nt, preferred_element_type=F32)
-        peak = jnp.maximum(jnp.max(s0, -1, keepdims=True), jnp.max(s1, -1, keepdims=True))
-        e0 = jnp.exp2((s0 - peak) * EXP2)
-        e1 = jnp.exp2((s1 - peak) * EXP2)
-        total = jnp.sum(e0, -1, keepdims=True) + jnp.sum(e1, -1, keepdims=True)
-        o = jnp.dot(e0.astype(BF16), v0_ref[:, cut], preferred_element_type=F32)
-        o = o + jnp.dot(e1.astype(BF16), v1_ref[:, cut], preferred_element_type=F32)
-        o = o / total
-        out_ref[:, k * KROWS : (k + 1) * KROWS, :] = o.astype(BF16).reshape(reqs, KROWS, HD)
-        peaks.append(peak * SCALE)
-        totals.append(total)
     row = lax.broadcasted_iota(jnp.int32, (KROWS, HD), 0)
     lane = lax.broadcasted_iota(jnp.int32, (KROWS, HD), 1)
-    place = lax.broadcasted_iota(jnp.int32, (16, HD), 0)
-    for r in range(reqs):
-        cut = slice(r * KROWS, (r + 1) * KROWS)
-        lines = []
-        for parts in (peaks, totals):
-            line = jnp.zeros((1, HD), F32)
-            for k in range(HALF_KV):
-                spread = jnp.where(lane == row + k * KROWS, parts[k][cut], 0.0)
-                line = line + jnp.sum(spread, 0, keepdims=True)
-            lines.extend(three(line))
-        stats = jnp.zeros((16, HD), F32)
-        for i, line in enumerate(lines):
-            stats = jnp.where(place == i, line, stats)
-        out_ref[r, HROWS:PAY, :] = stats.astype(BF16)
-
-
-def attend(q, k0, v0, k1, v1):
+    place = lax.broadcasted_iota(jnp.int32, (8, HD), 0)
+    size = k_hbm.shape[1] // CHUNKS
+    fetches = []
+    for k in range(HALF_KV):
+        for kind, (source, target) in enumerate(((k_hbm, k_ref), (v_hbm, v_ref))):
+            for c in range(CHUNKS):
+                at = pl.ds(c * size, size)
+                slot = (k * 2 + kind) * CHUNKS + c
+                fetches.append(pltpu.make_async_copy(source.at[k, at], target.at[k, at], sem.at[slot]))
+    for fetch in fetches:
+        fetch.start()
+
+    for k in range(HALF_KV):
+        for fetch in fetches[k * 2 * CHUNKS : (k + 1) * 2 * CHUNKS]:
+            fetch.wait()
+
+        def group(g, k=k):
+            base = g * per
+            rows = slice(k * KROWS, (k + 1) * KROWS)
+            q = q_ref[pl.ds(base, per), rows, :].reshape(per * KROWS, HD)
+            width = k_hbm.shape[1] // CHUNKS
+
+            def score(c):
+                return lax.dot_general(q, k_ref[k, c * width : (c + 1) * width, :], nt, preferred_element_type=F32)
+
+            ahead = score(0)
+            for c in range(CHUNKS):
+                s = ahead
+                if c + 1 < CHUNKS:
+                    ahead = score(c + 1)
+                best = jnp.max(s, -1, keepdims=True)
+                if c:
+                    best = jnp.maximum(peak, best)
+                    keep = jnp.exp2((peak - best) * EXP2)
+                e = jnp.exp2((s - best) * EXP2)
+                here = jnp.sum(e, -1, keepdims=True)
+                o = jnp.dot(e.astype(BF16), v_ref[k, c * width : (c + 1) * width, :], preferred_element_type=F32)
+                total = total * keep + here if c else here
+                acc = acc * keep + o if c else o
+                peak = best
+            o = acc / total
+            out_ref[pl.ds(base, per), rows, :] = o.astype(BF16).reshape(per, KROWS, HD)
+            peak = peak * SCALE
+            for r in range(per):
+                cut = slice(r * KROWS, (r + 1) * KROWS)
+                stats = jnp.zeros((8, HD), F32)
+                for i, part in enumerate((peak, total)):
+                    spread = jnp.where(lane == row + k * KROWS, part[cut], 0.0)
+                    for j, line in enumerate(three(jnp.sum(spread, 0, keepdims=True))):
+                        stats = jnp.where(place == 3 * i + j, line, stats)
+                if k == 0:
+                    stat_ref[base + r] = stats
+                else:
+                    out_ref[base + r, HROWS:PAY, :] = (stat_ref[base + r] + stats).astype(BF16)
+
+        pl.loop(0, q_ref.shape[0] // per)(group)
+
+
+def attend(q, keys, values):
     count = q.shape[0]
-    pre_rows = k0.shape[0]
-    per = math.gcd(count, 4)
-    fixed = lambda i: (0, 0)
-    kv = pl.BlockSpec((pre_rows, WIDE), fixed)
+    rows = keys.shape[1]
+    vmem = pl.BlockSpec(memory_space=pltpu.VMEM)
+    hbm = pl.BlockSpec(memory_space=pl.ANY)
     return pl.pallas_call(
-        attend_kernel,
+        functools.partial(attend_kernel, math.gcd(count, Q_GROUP)),
         out_shape=jax.ShapeDtypeStruct((count, PAY, HD), BF16),
-        grid=(count // per,),
-        in_specs=[pl.BlockSpec((per, HROWS, HD), lambda i: (i, 0, 0)), kv, kv, kv, kv],
-        out_specs=pl.BlockSpec((per, PAY, HD), lambda i: (i, 0, 0)),
-        compiler_params=pltpu.CompilerParams(vmem_limit_bytes=40 << 20),
+        in_specs=[vmem, hbm, hbm],
+        out_specs=vmem,
+        scratch_shapes=[
+            pltpu.VMEM((HALF_KV, rows, HD), BF16),
+            pltpu.VMEM((HALF_KV, rows, HD), BF16),
+            pltpu.VMEM((count, 8, HD), F32),
+            pltpu.SemaphoreType.DMA((4 * CHUNKS,)),
+        ],
+        compiler_params=pltpu.CompilerParams(vmem_limit_bytes=48 << 20),
         cost_estimate=pl.CostEstimate(
-            flops=8 * count * HROWS * HD * pre_rows,
-            bytes_accessed=8 * pre_rows * WIDE,
-            transcendentals=2 * count * HROWS * pre_rows,
+            flops=4 * count * HROWS * HD * rows,
+            bytes_accessed=4 * rows * WIDE,
+            transcendentals=count * HROWS * rows,
         ),
         name="attend",
-    )(q, k0, v0, k1, v1)
+    )(q, far(keys), far(values))
 
 
 def suffix_kernel(len_ref, q_ref, nk_ref, nv_ref, k_ref, v_ref, acc_ref, peak_ref, total_ref):
@@ -332,8 +421,9 @@
         cost_estimate=pl.CostEstimate(
             flops=4 * ROWS * SUF * HD, bytes_accessed=4 * SUF * KVH * HD, transcendentals=ROWS * SUF
         ),
+        compiler_params=pltpu.CompilerParams(vmem_limit_bytes=40 << 20),
         name="suffix",
-    )(length, q, new_rot, new_values, keys, values)
+    )(length, q, new_rot, new_values, far(keys), far(values))
 
 
 def combine_kernel(got_ref, acc_ref, peak_ref, total_ref, out_ref):
@@ -377,6 +467,7 @@
         out_shape=jax.ShapeDtypeStruct((1, STEPS, QH * HD), BF16),
         in_specs=[vmem] * 4,
         out_specs=vmem,
+        compiler_params=pltpu.CompilerParams(vmem_limit_bytes=8 << 20),
         name="combine",
     )(got, acc, peak, total)
 
@@ -400,10 +491,10 @@
     send, own, new_rot = rotate_queries(queries, new_keys, suffix_len, prefix, count)
     other_latent = lax.ppermute(prefix_latent, "seq", swap)
     other_order = lax.ppermute(block_order, "seq", swap)
+    send, other_order = lax.optimization_barrier((send, other_order))
     gathered = lax.all_to_all(send, "seq", split_axis=0, concat_axis=0, tiled=True)
-    k0, v0 = project(core, block_order, prefix_latent, key_up, value_up)
-    k1, v1 = project(core, other_order, other_latent, key_up, value_up)
-    parts = attend(gathered, k0, v0, k1, v1)
+    keys, values = project(core, block_order, other_order, prefix_latent, other_latent, key_up, value_up)
+    parts = attend(gathered, keys, values)
     got = lax.all_to_all(parts, "seq", split_axis=0, concat_axis=0, tiled=True)
     new_pad = jnp.pad(new_values[0], ((0, 16 - STEPS), (0, 0)))
     acc, peak, total = suffix(suffix_len, own, new_rot, new_pad, suffix_keys, suffix_values)

time: 55.8 us -> 44.9 us (0.80)
  local copies, waits for them, and re-layouts: 7.99 us -> 0.02 us
  Pallas kernels: 25.8 us -> 21.9 us
  waiting for transfers between devices: 6.92 us -> 10.5 us
  starting transfers between devices: 13.7 us -> 11.2 us
    unnamed x16 -> x8, local copies, waits for them, and re-layouts: 7.39 us -> 0.01 us
    pallas_call x3 -> x2, Pallas kernels: 18.8 us -> 15.7 us  [the longest x1 8.13 us: attend(): pl.pallas_call(functools.partial(attend_kernel, math.gcd(count, Q_GROUP))...]
    all_to_all x1, waiting for transfers between devices: 0.01 us -> 2.41 us  [local(): lax.all_to_all(send, 'seq', split_axis=0, concat_axis=0, tiled=True)]
    all_to_all x1, starting transfers between devices: 5.77 us -> 3.64 us  [local(): got = lax.all_to_all(parts, 'seq', split_axis=0, concat_axis=0, tiled=True)]
    ppermute x1, waiting for transfers between devices: 0.01 us -> 1.32 us  [local(): other_order = lax.ppermute(block_order, 'seq', swap)]
    pallas_call x1, Pallas kernels: 1.9 us -> 0.89 us  [combine(): pl.pallas_call(combine_kernel, out_shape=jax.ShapeDtypeStruct((1, STEPS,...]
    pad x1, local copies, waits for them, and re-layouts: 0.6 us -> 0.01 us  [local(): new_pad = jnp.pad(new_values[0], ((0, 16 - STEPS), (0, 0)))]
  transfers between devices with their start and end apart: 4 -> 4, of which waited for: 1 -> 3; matrix products, arithmetic and copies ran while one was open for 1% -> 0% of each run, Pallas kernels for 28% -> 29%
where the time goes in v2:
time: 44.9 us; the launch traced here: 44.4 us
  Pallas kernels  21.9 us (49%)
  starting transfers between devices  11.2 us (25%)
  waiting for transfers between devices  10.5 us (23%)
  between operations  0.75 us (2%)
    pallas_call x1, Pallas kernels, attend(): pl.pallas_call(functools.partial(attend_kernel, math.gcd(count, Q_GROUP))...  8.13 us
    pallas_call x1, Pallas kernels, project(): pl.pallas_call(project_kernel, out_shape=(out, out), in_specs=[smem, smem...  7.6 us
    all_to_all x1, starting transfers between devices, local(): lax.all_to_all(send, 'seq', split_axis=0, concat_axis=0, tiled=True)  7.05 us
    all_to_all x1, waiting for transfers between devices, local(): got = lax.all_to_all(parts, 'seq', split_axis=0, concat_axis=0, tiled=True)  6.81 us
    pallas_call x1, Pallas kernels, suffix(): pl.pallas_call(suffix_kernel, out_shape=(out, out, out), grid_spec=pltpu....  3.71 us
    all_to_all x1, starting transfers between devices, local(): got = lax.all_to_all(parts, 'seq', split_axis=0, concat_axis=0, tiled=True)  3.64 us
    all_to_all x1, waiting for transfers between devices, local(): lax.all_to_all(send, 'seq', split_axis=0, concat_axis=0, tiled=True)  2.41 us
    pallas_call x1, Pallas kernels, rotate_queries(): pl.pallas_call(functools.partial(query_kernel, prefix, count), out_shape=...  1.58 us
  transfers between devices with their start and end apart: 4, of which 3 were waited for; matrix products, arithmetic and copies ran while one was open for 0% of the time, Pallas kernels for 29%

profile of v2, /device:TPU:0, one launch (start us, length us, event | category | flops | bytes accessed | tf_op | source)
XLA Modules:
  0.0 44.4 jit_solution(15689023973557765160)
XLA Ops:
  0.0 0.5 %collective-permute-start.1 = (bf16[1920,512]{1,0:T(8,128)(2,1)}, bf16[1920,512]{1,0:T(8,128)(2,1)}, u32[]{:S(2)}, u32[]{:S(2)}) collective-permute-start(bf16[1920,512]{1,0:T(8,128)(2,1)} %lat0_hbm.1), channel_id=1, source_target_pairs={{0,1},{1,0},{2,3},{3,2},{4,5},{5,4},{6,7},{7,6},{8,9},{9,8},{10,11... | collective-permute-start | bytes 5898248 | tf_op jit(solution)/shard_map/ppermute | solution.py:492
  0.5 0.1 collective-permute-start
  1.2 1.6 %rotate_queries.1 = (bf16[16,64,128]{2,1,0:T(8,128)(2,1)}, bf16[128,128]{1,0:T(8,128)(2,1)}, bf16[16,512]{1,0:T(8,128)(2,1)}) custom-call(s32[1]{0:T(128)S(6)} %copy.15.len_ref, s32[8,128]{1,0:T(8,128)} %constant.26.clone.table_ref, bf16[1,4,4096]{2,1,0:T(4,128)(2,1)} %q_ref.1, bf16[1,4,512]{2,1,0:T(4,128)(2,1)} %nk_ref.1), custom_call_target="tpu_custom_call" | custom-call | tf_op jit(solution)/shard_map/rotate_queries/pallas_call | solution.py:103
  2.7 1.3 %collective-permute-done.order1_ref = s32[15]{0:T(128)S(1)} collective-permute-done((s32[15]{0:T(128)}, s32[15]{0:T(128)S(1)}, u32[]{:S(2)}, u32[]{:S(2)}) %collective-permute-start) | collective-permute-done | bytes 92 | tf_op jit(solution)/shard_map/ppermute | solution.py:493
  4.1 0.0 copy-start.3
  4.1 7.1 %all-to-all-start = ((bf16[16,64,128]{2,1,0:T(8,128)(2,1)}), bf16[16,64,128]{2,1,0:T(8,128)(2,1)S(1)}, u32[]{:S(2)}, u32[]{:S(2)}) async-start(bf16[16,64,128]{2,1,0:T(8,128)(2,1)} %get-tuple-element.16), calls=%async_computation | async-start | bytes 524288 | tf_op jit(solution)/shard_map/all_to_all | solution.py:495
  11.1 0.0 collective-permute-done.1.lat1_hbm
  11.2 0.0 copy-done.3
  11.2 7.6 %project.1 = (bf16[2,3840,128]{2,1,0:T(8,128)(2,1)}, bf16[2,3840,128]{2,1,0:T(8,128)(2,1)}) custom-call(s32[1]{0:T(128)} %bitcast.core_ref, s32[15]{0:T(128)} %order0_ref.1, s32[15]{0:T(128)} %copy-done.3, bf16[1920,512]{1,0:T(8,128)(2,1)} %lat0_hbm.1, bf16[1920,512]{1,0:T(8,128)(2,1)} %collective-permute-done.1.lat1_hbm, bf16[512,512]{1,0:T(8,128)(2,1)} %ku_hbm.1, ...), custom_call_target="tpu_custom_call" | custom-call | flops 2013265920 | bytes 7864320 | tf_op jit(solution)/shard_map/project/pallas_call | solution.py:213
  18.8 2.4 %all-to-all-done.q_ref = bf16[16,64,128]{2,1,0:T(8,128)(2,1)S(1)} async-done(((bf16[16,64,128]{2,1,0:T(8,128)(2,1)}), bf16[16,64,128]{2,1,0:T(8,128)(2,1)S(1)}, u32[]{:S(2)}, u32[]{:S(2)}) %all-to-all-start) | async-done | bytes 262176 | tf_op jit(solution)/shard_map/all_to_all | solution.py:495
  21.2 0.0 copy-start.2
  21.2 0.0 copy-start
  21.2 0.0 copy-start.1
  21.2 8.1 %attend.1 = bf16[16,72,128]{2,1,0:T(8,128)(2,1)} custom-call(bf16[16,64,128]{2,1,0:T(8,128)(2,1)S(1)} %all-to-all-done.q_ref, bf16[2,3840,128]{2,1,0:T(8,128)(2,1)} %get-tuple-element.18.k_hbm, bf16[2,3840,128]{2,1,0:T(8,128)(2,1)} %get-tuple-element.19.v_hbm), custom_call_target="tpu_custom_call" | custom-call | flops 2013265920 | bytes 3932160 | tf_op jit(solution)/shard_map/attend/pallas_call | solution.py:316
  29.3 3.6 %all-to-all-start.1 = ((bf16[16,72,128]{2,1,0:T(8,128)(2,1)}), bf16[16,72,128]{2,1,0:T(8,128)(2,1)S(1)}, u32[]{:S(2)}, u32[]{:S(2)}) async-start(bf16[16,72,128]{2,1,0:T(8,128)(2,1)} %attend.1), calls=%async_computation.1 | async-start | bytes 589824 | tf_op jit(solution)/shard_map/all_to_all | solution.py:498
  33.0 0.0 copy-done.2
  33.0 0.0 copy-done
  33.0 0.0 copy-done.1
  33.0 3.7 %suffix.1 = (f32[128,128]{1,0:T(8,128)S(1)}, f32[128,128]{1,0:T(8,128)S(1)}, f32[128,128]{1,0:T(8,128)S(1)}) custom-call(s32[1]{0:T(128)S(6)} %copy.15.len_ref, bf16[128,128]{1,0:T(8,128)(2,1)S(1)} %copy-done, bf16[16,512]{1,0:T(8,128)(2,1)S(1)} %copy-done.1, bf16[16,512]{1,0:T(8,128)(2,1)S(1)} %pad.4.nv_ref, bf16[1,4096,512]{2,1,0:T(8,128)(2,1)} %k_ref.1, ...), custom_call_target="tpu_custom_call" | custom-call | flops 268435456 | bytes 8388608 | tf_op jit(solution)/shard_map/suffix/pallas_call | solution.py:406
  36.7 6.8 %all-to-all-done.1.got_ref = bf16[16,72,128]{2,1,0:T(8,128)(2,1)S(1)} async-done(((bf16[16,72,128]{2,1,0:T(8,128)(2,1)}), bf16[16,72,128]{2,1,0:T(8,128)(2,1)S(1)}, u32[]{:S(2)}, u32[]{:S(2)}) %all-to-all-start.1) | async-done | bytes 294944 | tf_op jit(solution)/shard_map/all_to_all | solution.py:498
  43.5 0.9 %combine.1 = bf16[1,4,4096]{2,1,0:T(4,128)(2,1)} custom-call(bf16[16,72,128]{2,1,0:T(8,128)(2,1)S(1)} %all-to-all-done.1.got_ref, f32[128,128]{1,0:T(8,128)S(1)} %get-tuple-element.22.acc_ref, f32[128,128]{1,0:T(8,128)S(1)} %get-tuple-element.23.peak_ref, f32[128,128]{1,0:T(8,128)S(1)} %get-tuple-element.24.total_ref), custom_call_target="tpu_custom_call" | custom-call | tf_op jit(solution)/shard_map/combine/pallas_call | solution.py:465
  (1 shorter events, 0.0 us)
Async XLA Ops:
  0.0 11.1 %collective-permute-start.1 = (bf16[1920,512]{1,0:T(8,128)(2,1)}, bf16[1920,512]{1,0:T(8,128)(2,1)}, u32[]{:S(2)}, u32[]{:S(2)}) collective-permute-start(bf16[1920,512]{1,0:T(8,128)(2,1)} %lat0_hbm.1), channel_id=1, source_target_pairs={{0,1},{1,0},{2,3},{3,2},{4,5},{5,4},{6,7},{7,6},{8,9},{9,8},{10,11... | collective-permute-start | bytes 5898248 | tf_op jit(solution)/shard_map/ppermute | solution.py:492
  0.5 3.6 %collective-permute-start = (s32[15]{0:T(128)}, s32[15]{0:T(128)S(1)}, u32[]{:S(2)}, u32[]{:S(2)}) collective-permute-start(s32[15]{0:T(128)} %order0_ref.1), channel_id=1, source_target_pairs={{0,1},{1,0},{2,3},{3,2},{4,5},{5,4},{6,7},{7,6},{8,9},{9,8},{10,11... | collective-permute-start | bytes 188 | tf_op jit(solution)/shard_map/ppermute | solution.py:493
  4.1 7.1 %copy-start.3 = (s32[15]{0:T(128)}, s32[15]{0:T(128)S(1)}, u32[]{:S(2)}) copy-start(s32[15]{0:T(128)S(1)} %collective-permute-done.order1_ref) | copy-start | bytes 184
  4.1 17.1 %all-to-all-start = ((bf16[16,64,128]{2,1,0:T(8,128)(2,1)}), bf16[16,64,128]{2,1,0:T(8,128)(2,1)S(1)}, u32[]{:S(2)}, u32[]{:S(2)}) async-start(bf16[16,64,128]{2,1,0:T(8,128)(2,1)} %get-tuple-element.16), calls=%async_computation | async-start | bytes 524288 | tf_op jit(solution)/shard_map/all_to_all | solution.py:495
  21.2 11.8 %copy-start.2 = (bf16[1,4,512]{2,1,0:T(4,128)(2,1)S(1)}, bf16[1,4,512]{2,1,0:T(4,128)(2,1)}, u32[]{:S(2)}) copy-start(bf16[1,4,512]{2,1,0:T(4,128)(2,1)} %param.20) | copy-start | bytes 12292
  21.2 11.8 %copy-start = (bf16[128,128]{1,0:T(8,128)(2,1)S(1)}, bf16[128,128]{1,0:T(8,128)(2,1)}, u32[]{:S(2)}) copy-start(bf16[128,128]{1,0:T(8,128)(2,1)} %get-tuple-element.20.q_ref) | copy-start | bytes 98308
  21.2 11.8 %copy-start.1 = (bf16[16,512]{1,0:T(8,128)(2,1)S(1)}, bf16[16,512]{1,0:T(8,128)(2,1)}, u32[]{:S(2)}) copy-start(bf16[16,512]{1,0:T(8,128)(2,1)} %get-tuple-element.21.nk_ref) | copy-start | bytes 49156
  29.3 14.2 %all-to-all-start.1 = ((bf16[16,72,128]{2,1,0:T(8,128)(2,1)}), bf16[16,72,128]{2,1,0:T(8,128)(2,1)S(1)}, u32[]{:S(2)}, u32[]{:S(2)}) async-start(bf16[16,72,128]{2,1,0:T(8,128)(2,1)} %attend.1), calls=%async_computation.1 | async-start | bytes 589824 | tf_op jit(solution)/shard_map/all_to_all | solution.py:498

commit v3 on v2

--- a/solution.py
+++ b/solution.py
@@ -24,10 +24,9 @@
 PAY = HROWS + 8
 SCALE = 1.0 / math.sqrt(HD)
 EXP2 = SCALE * math.log2(math.e)
-LOG2E = math.log2(math.e)
 TURN = 2.0 * math.pi / 16777216.0
 SUF_TILE = 1024
-PER = 5
+PER = 15
 Q_GROUP = 16
 CHUNKS = 5
 F32 = jnp.float32
@@ -75,7 +74,7 @@
 
 def query_kernel(prefix, count, len_ref, table_ref, q_ref, nk_ref, send_ref, own_ref, new_ref, rows_ref, nrows_ref):
     step = lax.broadcasted_iota(jnp.int32, (8, HD), 0) % STEPS
-    spot = prefix + len_ref[0] + step
+    spot = prefix + jnp.broadcast_to(len_ref[...][None], (8, HD)) + step
     angle = phases(spot, table_ref[0:1, :], table_ref[1:2, :])
     cosine = jnp.cos(angle)
     sine = jnp.sin(angle) * lane_sign((8, HD))
@@ -98,7 +97,6 @@
 
 
 def rotate_queries(queries, new_keys, suffix_len, prefix, count):
-    smem = pl.BlockSpec(memory_space=pltpu.SMEM)
     vmem = pl.BlockSpec(memory_space=pltpu.VMEM)
     return pl.pallas_call(
         functools.partial(query_kernel, prefix, count),
@@ -107,7 +105,7 @@
             jax.ShapeDtypeStruct((ROWS, HD), BF16),
             jax.ShapeDtypeStruct((16, KVH * HD), BF16),
         ),
-        in_specs=[smem, vmem, vmem, vmem],
+        in_specs=[vmem] * 4,
         out_specs=(vmem, vmem, vmem),
         scratch_shapes=[pltpu.VMEM((ROWS, HD), F32), pltpu.VMEM((16, KVH * HD), F32)],
         name="rotate_queries",
@@ -125,13 +123,15 @@
     table_ref,
     rc_ref,
     rs_ref,
+    k0_ref,
+    v0_hbm,
     k_hbm,
     v_hbm,
     bc_ref,
     bs_ref,
     lat_ref,
-    ku_ref,
-    vu_ref,
+    w_ref,
+    v0_ref,
     k_ref,
     v_ref,
     in_sem,
@@ -145,8 +145,8 @@
     size = per * BLK
     mine = pl.ds(pl.multiple_of(core_ref[0] * WIDE, WIDE), WIDE)
     loads = [
-        pltpu.make_async_copy(ku_hbm.at[:, mine], ku_ref, w_sem.at[0]),
-        pltpu.make_async_copy(vu_hbm.at[:, mine], vu_ref, w_sem.at[1]),
+        pltpu.make_async_copy(ku_hbm.at[:, mine], w_ref.at[:, 0:WIDE], w_sem.at[0]),
+        pltpu.make_async_copy(vu_hbm.at[:, mine], w_ref.at[:, WIDE : 2 * WIDE], w_sem.at[1]),
     ]
     fetches = []
     for side, source in enumerate((lat0_hbm, lat1_hbm)):
@@ -160,11 +160,13 @@
     for fetch in fetches[1:]:
         fetch.start()
     pad = bc_ref.shape[0]
-    row = lax.broadcasted_iota(jnp.int32, (pad, HD), 0)
-    spot = jnp.zeros((pad, HD), jnp.int32)
+    narrow = lax.broadcasted_iota(jnp.int32, (pad, blocks), 1)
+    tall = lax.broadcasted_iota(jnp.int32, (pad, blocks), 0)
+    spot = jnp.zeros((pad, 1), F32)
     for side, order_ref in enumerate((order0_ref, order1_ref)):
-        for b in range(blocks):
-            spot = jnp.where(row == side * blocks + b, order_ref[b], spot)
+        order = jnp.broadcast_to(order_ref[...].astype(F32), (pad, blocks))
+        spot = spot + jnp.sum(jnp.where(tall == side * blocks + narrow, order, 0.0), -1, keepdims=True)
+    spot = jnp.broadcast_to(spot.astype(jnp.int32), (pad, HD))
     angle = phases(spot * BLK, table_ref[0:1, :], table_ref[1:2, :])
     bc_ref[...] = jnp.cos(angle)
     bs_ref[...] = jnp.sin(angle) * lane_sign((pad, HD))
@@ -175,25 +177,23 @@
         at = pl.ds(slot * size, size)
         fetches[slot].wait()
         lat = lat_ref[at, :]
-        keys = jnp.dot(lat, ku_ref[...], preferred_element_type=F32)
-        values = jnp.dot(lat, vu_ref[...], preferred_element_type=F32).astype(BF16)
-        for k in range(HALF_KV):
-            v_ref[k, at, :] = values[:, k * HD : (k + 1) * HD]
+        keys = jnp.dot(lat, w_ref[...], preferred_element_type=F32)
+        values = keys[:, WIDE:].astype(BF16)
+        for target, k in ((v0_ref, 0), (v_ref, 1)):
+            target[at, :] = values[:, k * HD : (k + 1) * HD]
         for i in range(per):
             b = slot * per + i
             block_cos = bc_ref[b : b + 1, :]
             block_sin = bs_ref[b : b + 1, :]
             cosine = block_cos * rc_ref[...] - block_sin * rs_ref[...]
             sine = block_sin * rc_ref[...] + block_cos * rs_ref[...]
-            for k in range(HALF_KV):
+            for target, k in ((k0_ref, 0), (k_ref, 1)):
                 part = keys[i * BLK : (i + 1) * BLK, k * HD : (k + 1) * HD]
-                k_ref[k, b * BLK : (b + 1) * BLK, :] = turn(part, cosine, sine).astype(BF16)
-        for k in range(HALF_KV):
-            for kind, (source, target) in enumerate(((k_ref, k_hbm), (v_ref, v_hbm))):
-                sem = out_sem.at[(slot * HALF_KV + k) * 2 + kind]
-                store = pltpu.make_async_copy(source.at[k, at], target.at[k, at], sem)
-                store.start()
-                stores.append(store)
+                target[b * BLK : (b + 1) * BLK, :] = turn(part, cosine, sine).astype(BF16)
+        for kind, (source, target) in enumerate(((v0_ref, v0_hbm), (k_ref, k_hbm), (v_ref, v_hbm))):
+            store = pltpu.make_async_copy(source.at[at], target.at[at], out_sem.at[slot * 3 + kind])
+            store.start()
+            stores.append(store)
     for store in stores:
         store.wait()
 
@@ -209,30 +209,42 @@
     vmem = pl.BlockSpec(memory_space=pltpu.VMEM)
     hbm = pl.BlockSpec(memory_space=pl.ANY)
     pad = -(-2 * blocks // 8) * 8
-    out = jax.ShapeDtypeStruct((HALF_KV, rows, HD), BF16)
+    out = jax.ShapeDtypeStruct((rows, HD), BF16)
+    out_far = pltpu.HBM((rows, HD), BF16)
     return pl.pallas_call(
         project_kernel,
-        out_shape=(out, out),
-        in_specs=[smem, smem, smem, hbm, hbm, hbm, hbm, vmem, vmem, vmem],
-        out_specs=(hbm, hbm),
+        out_shape=(out, out_far, out_far, out_far),
+        in_specs=[smem, vmem, vmem, hbm, hbm, hbm, hbm, vmem, vmem, vmem],
+        out_specs=(vmem, hbm, hbm, hbm),
         scratch_shapes=[
             pltpu.VMEM((pad, HD), F32),
             pltpu.VMEM((pad, HD), F32),
             pltpu.VMEM((rows, rank), BF16),
-            pltpu.VMEM((rank, WIDE), BF16),
-            pltpu.VMEM((rank, WIDE), BF16),
-            pltpu.VMEM((HALF_KV, rows, HD), BF16),
-            pltpu.VMEM((HALF_KV, rows, HD), BF16),
+            pltpu.VMEM((rank, 2 * WIDE), BF16),
+            pltpu.VMEM((rows, HD), BF16),
+            pltpu.VMEM((rows, HD), BF16),
+            pltpu.VMEM((rows, HD), BF16),
             pltpu.SemaphoreType.DMA((slots,)),
             pltpu.SemaphoreType.DMA((2,)),
-            pltpu.SemaphoreType.DMA((slots * HALF_KV * 2,)),
+            pltpu.SemaphoreType.DMA((slots * 3,)),
         ],
         cost_estimate=pl.CostEstimate(
             flops=4 * rows * rank * WIDE, bytes_accessed=rows * (rank + 2 * WIDE) * 2, transcendentals=0
         ),
-        compiler_params=pltpu.CompilerParams(vmem_limit_bytes=(64 << 20) - 2200000),
+        compiler_params=pltpu.CompilerParams(vmem_limit_bytes=40 << 20),
         name="project",
-    )(core, order0, order1, far(latent0), latent1, far(key_up), far(value_up), jnp.asarray(phase_rows()), jnp.asarray(rc), jnp.asarray(rs))
+    )(
+        core,
+        far(order0[None]),
+        order1[None],
+        far(latent0),
+        latent1,
+        far(key_up),
+        far(value_up),
+        far(jnp.asarray(phase_rows())),
+        far(jnp.asarray(rc)),
+        far(jnp.asarray(rs)),
+    )
 
 
 def far(x):
@@ -246,34 +258,33 @@
     return first, second, rest - second
 
 
-def attend_kernel(per, q_ref, k_hbm, v_hbm, out_ref, k_ref, v_ref, stat_ref, sem):
+def attend_kernel(per, q_ref, k0_ref, v0_hbm, k_hbm, v_hbm, out_ref, v0_ref, k_ref, v_ref, stat_ref, sem):
     nt = (((1,), (1,)), ((), ()))
     row = lax.broadcasted_iota(jnp.int32, (KROWS, HD), 0)
     lane = lax.broadcasted_iota(jnp.int32, (KROWS, HD), 1)
     place = lax.broadcasted_iota(jnp.int32, (8, HD), 0)
-    size = k_hbm.shape[1] // CHUNKS
-    fetches = []
-    for k in range(HALF_KV):
-        for kind, (source, target) in enumerate(((k_hbm, k_ref), (v_hbm, v_ref))):
-            for c in range(CHUNKS):
-                at = pl.ds(c * size, size)
-                slot = (k * 2 + kind) * CHUNKS + c
-                fetches.append(pltpu.make_async_copy(source.at[k, at], target.at[k, at], sem.at[slot]))
+    fetches = [
+        pltpu.make_async_copy(v0_hbm, v0_ref, sem.at[0]),
+        pltpu.make_async_copy(k_hbm, k_ref, sem.at[1]),
+        pltpu.make_async_copy(v_hbm, v_ref, sem.at[2]),
+    ]
     for fetch in fetches:
         fetch.start()
 
     for k in range(HALF_KV):
-        for fetch in fetches[k * 2 * CHUNKS : (k + 1) * 2 * CHUNKS]:
-            fetch.wait()
-
-        def group(g, k=k):
+        if k:
+            fetches[1].wait()
+            fetches[2].wait()
+        keys, values = ((k0_ref, v0_ref), (k_ref, v_ref))[k]
+
+        def group(g, first=False, k=k, keys=keys, values=values):
             base = g * per
             rows = slice(k * KROWS, (k + 1) * KROWS)
             q = q_ref[pl.ds(base, per), rows, :].reshape(per * KROWS, HD)
-            width = k_hbm.shape[1] // CHUNKS
+            width = k_hbm.shape[0] // CHUNKS
 
             def score(c):
-                return lax.dot_general(q, k_ref[k, c * width : (c + 1) * width, :], nt, preferred_element_type=F32)
+                return lax.dot_general(q, keys[c * width : (c + 1) * width, :], nt, preferred_element_type=F32)
 
             ahead = score(0)
             for c in range(CHUNKS):
@@ -281,18 +292,20 @@
                 if c + 1 < CHUNKS:
                     ahead = score(c + 1)
                 best = jnp.max(s, -1, keepdims=True)
+                if first and c == 0:
+                    fetches[0].wait()
                 if c:
                     best = jnp.maximum(peak, best)
                     keep = jnp.exp2((peak - best) * EXP2)
                 e = jnp.exp2((s - best) * EXP2)
                 here = jnp.sum(e, -1, keepdims=True)
-                o = jnp.dot(e.astype(BF16), v_ref[k, c * width : (c + 1) * width, :], preferred_element_type=F32)
+                o = jnp.dot(e.astype(BF16), values[c * width : (c + 1) * width, :], preferred_element_type=F32)
                 total = total * keep + here if c else here
                 acc = acc * keep + o if c else o
                 peak = best
             o = acc / total
             out_ref[pl.ds(base, per), rows, :] = o.astype(BF16).reshape(per, KROWS, HD)
-            peak = peak * SCALE
+            peak = peak * EXP2
             for r in range(per):
                 cut = slice(r * KROWS, (r + 1) * KROWS)
                 stats = jnp.zeros((8, HD), F32)
@@ -305,24 +318,28 @@
                 else:
                     out_ref[base + r, HROWS:PAY, :] = (stat_ref[base + r] + stats).astype(BF16)
 
-        pl.loop(0, q_ref.shape[0] // per)(group)
-
-
-def attend(q, keys, values):
+        group(0, k == 0)
+        groups = q_ref.shape[0] // per
+        if groups > 1:
+            pl.loop(1, groups)(group)
+
+
+def attend(q, k0, v0, k1, v1):
     count = q.shape[0]
-    rows = keys.shape[1]
+    rows = k0.shape[0]
     vmem = pl.BlockSpec(memory_space=pltpu.VMEM)
     hbm = pl.BlockSpec(memory_space=pl.ANY)
     return pl.pallas_call(
         functools.partial(attend_kernel, math.gcd(count, Q_GROUP)),
         out_shape=jax.ShapeDtypeStruct((count, PAY, HD), BF16),
-        in_specs=[vmem, hbm, hbm],
+        in_specs=[vmem, vmem, hbm, hbm, hbm],
         out_specs=vmem,
         scratch_shapes=[
-            pltpu.VMEM((HALF_KV, rows, HD), BF16),
-            pltpu.VMEM((HALF_KV, rows, HD), BF16),
+            pltpu.VMEM((rows, HD), BF16),
+            pltpu.VMEM((rows, HD), BF16),
+            pltpu.VMEM((rows, HD), BF16),
             pltpu.VMEM((count, 8, HD), F32),
-            pltpu.SemaphoreType.DMA((4 * CHUNKS,)),
+            pltpu.SemaphoreType.DMA((3,)),
         ],
         compiler_params=pltpu.CompilerParams(vmem_limit_bytes=48 << 20),
         cost_estimate=pl.CostEstimate(
@@ -331,7 +348,7 @@
             transcendentals=count * HROWS * rows,
         ),
         name="attend",
-    )(q, far(keys), far(values))
+    )(q, k0, far(v0), far(k1), far(v1))
 
 
 def suffix_kernel(len_ref, q_ref, nk_ref, nv_ref, k_ref, v_ref, acc_ref, peak_ref, total_ref):
@@ -395,7 +412,7 @@
 
     @pl.when(step == pl.num_programs(0) - 1)
     def _():
-        peak_ref[...] = peak_ref[...] * SCALE
+        peak_ref[...] = peak_ref[...] * EXP2
 
 
 def suffix(length, q, new_rot, new_values, keys, values):
@@ -441,7 +458,7 @@
         peaks = [s[0:1] + s[1:2] + s[2:3] for s in stats]
         totals = [s[3:4] + s[4:5] + s[5:6] for s in stats]
         top = functools.reduce(jnp.maximum, peaks)
-        factors = [t * jnp.exp2((p - top) * LOG2E) for p, t in zip(peaks, totals)]
+        factors = [t * jnp.exp2(p - top) for p, t in zip(peaks, totals)]
         denom = column(sum(factors))
         top = column(top)
         numer = jnp.zeros((HROWS, HD), F32)
@@ -450,8 +467,8 @@
         cut = slice(part * HROWS, (part + 1) * HROWS)
         near = peak_ref[cut, :]
         big = jnp.maximum(top, near)
-        far_weight = jnp.exp2((top - big) * LOG2E)
-        near_weight = jnp.exp2((near - big) * LOG2E)
+        far_weight = jnp.exp2(top - big)
+        near_weight = jnp.exp2(near - big)
         result = (numer * far_weight + acc_ref[cut, :] * near_weight) / (
             denom * far_weight + total_ref[cut, :] * near_weight
         )
@@ -491,10 +508,9 @@
     send, own, new_rot = rotate_queries(queries, new_keys, suffix_len, prefix, count)
     other_latent = lax.ppermute(prefix_latent, "seq", swap)
     other_order = lax.ppermute(block_order, "seq", swap)
-    send, other_order = lax.optimization_barrier((send, other_order))
     gathered = lax.all_to_all(send, "seq", split_axis=0, concat_axis=0, tiled=True)
-    keys, values = project(core, block_order, other_order, prefix_latent, other_latent, key_up, value_up)
-    parts = attend(gathered, keys, values)
+    projected = project(core, block_order, other_order, prefix_latent, other_latent, key_up, value_up)
+    parts = attend(gathered, *projected)
     got = lax.all_to_all(parts, "seq", split_axis=0, concat_axis=0, tiled=True)
     new_pad = jnp.pad(new_values[0], ((0, 16 - STEPS), (0, 0)))
     acc, peak, total = suffix(suffix_len, own, new_rot, new_pad, suffix_keys, suffix_values)

time: 44.9 us -> 42.7 us (0.951)
  waiting for transfers between devices: 10.5 us -> 7.57 us
    all_to_all x1, waiting for transfers between devices: 6.81 us -> 4.35 us  [local(): got = lax.all_to_all(parts, 'seq', split_axis=0, concat_axis=0, tiled=True)]
    pallas_call x1, Pallas kernels: 3.71 us -> 6.17 us  [suffix(): pl.pallas_call(suffix_kernel, out_shape=(out, out, out), grid_spec=pltpu....]
    pallas_call x1, Pallas kernels: 7.6 us -> 6.38 us  [project(): pl.pallas_call(project_kernel, out_shape=(out, out_far, out_far, out_far)...]
    pallas_call x1, Pallas kernels: 8.13 us -> 7.22 us  [attend(): pl.pallas_call(functools.partial(attend_kernel, math.gcd(count, Q_GROUP))...]
  transfers between devices with their start and end apart: 4 -> 4, of which waited for: 3 -> 3; matrix products, arithmetic and copies ran while one was open for 0% -> 0% of each run, Pallas kernels for 29% -> 34%
where the time goes in v3:
time: 42.7 us; the launch traced here: 42.2 us
  Pallas kernels  22.3 us (52%)
  starting transfers between devices  11.6 us (27%)
  waiting for transfers between devices  7.57 us (18%)
  between operations  0.75 us (2%)
    pallas_call x1, Pallas kernels, attend(): pl.pallas_call(functools.partial(attend_kernel, math.gcd(count, Q_GROUP))...  7.22 us
    all_to_all x1, starting transfers between devices, local(): lax.all_to_all(send, 'seq', split_axis=0, concat_axis=0, tiled=True)  7.05 us
    pallas_call x1, Pallas kernels, project(): pl.pallas_call(project_kernel, out_shape=(out, out_far, out_far, out_far)...  6.38 us
    pallas_call x1, Pallas kernels, suffix(): pl.pallas_call(suffix_kernel, out_shape=(out, out, out), grid_spec=pltpu....  6.17 us
    all_to_all x1, waiting for transfers between devices, local(): got = lax.all_to_all(parts, 'seq', split_axis=0, concat_axis=0, tiled=True)  4.35 us
    all_to_all x1, starting transfers between devices, local(): got = lax.all_to_all(parts, 'seq', split_axis=0, concat_axis=0, tiled=True)  3.65 us
    all_to_all x1, waiting for transfers between devices, local(): lax.all_to_all(send, 'seq', split_axis=0, concat_axis=0, tiled=True)  2.26 us
    pallas_call x1, Pallas kernels, rotate_queries(): pl.pallas_call(functools.partial(query_kernel, prefix, count), out_shape=...  1.64 us
  transfers between devices with their start and end apart: 4, of which 3 were waited for; matrix products, arithmetic and copies ran while one was open for 0% of the time, Pallas kernels for 34%

profile of v3, /device:TPU:0, one launch (start us, length us, event | category | flops | bytes accessed | tf_op | source)
XLA Modules:
  0.0 42.2 jit_solution(15523790903933537282)
XLA Ops:
  0.0 0.5 %collective-permute-start.1 = (bf16[1920,512]{1,0:T(8,128)(2,1)}, bf16[1920,512]{1,0:T(8,128)(2,1)S(1)}, u32[]{:S(2)}, u32[]{:S(2)}) collective-permute-start(bf16[1920,512]{1,0:T(8,128)(2,1)} %lat0_hbm.1), channel_id=1, source_target_pairs={{0,1},{1,0},{2,3},{3,2},{4,5},{5,4},{6,7},{7,6},{8,9},{9,8},{10,11... | collective-permute-start | bytes 5898248 | tf_op jit(solution)/shard_map/ppermute | solution.py:509
  1.1 1.6 %rotate_queries.1 = (bf16[16,64,128]{2,1,0:T(8,128)(2,1)}, bf16[128,128]{1,0:T(8,128)(2,1)}, bf16[16,512]{1,0:T(8,128)(2,1)}) custom-call(s32[1]{0:T(128)S(6)} %copy.15.len_ref, s32[8,128]{1,0:T(8,128)} %constant.26.clone.table_ref, bf16[1,4,4096]{2,1,0:T(4,128)(2,1)} %q_ref.1, bf16[1,4,512]{2,1,0:T(4,128)(2,1)} %nk_ref.1), custom_call_target="tpu_custom_call" | custom-call | tf_op jit(solution)/shard_map/rotate_queries/pallas_call | solution.py:101
  2.7 7.0 %all-to-all-start = ((bf16[16,64,128]{2,1,0:T(8,128)(2,1)}), bf16[16,64,128]{2,1,0:T(8,128)(2,1)S(1)}, u32[]{:S(2)}, u32[]{:S(2)}) async-start(bf16[16,64,128]{2,1,0:T(8,128)(2,1)} %get-tuple-element.15), calls=%async_computation | async-start | bytes 524288 | tf_op jit(solution)/shard_map/all_to_all | solution.py:511
  9.8 0.4 collective-permute-start
  10.2 1.0 %collective-permute-done = s32[15]{0:T(128)S(1)} collective-permute-done((s32[15]{0:T(128)}, s32[15]{0:T(128)S(1)}, u32[]{:S(2)}, u32[]{:S(2)}) %collective-permute-start) | collective-permute-done | bytes 92 | tf_op jit(solution)/shard_map/ppermute | solution.py:510
  11.2 0.0 collective-permute-done.1.lat1_hbm
  11.2 6.4 %project.1 = (bf16[3840,128]{1,0:T(8,128)(2,1)S(1)}, bf16[3840,128]{1,0:T(8,128)(2,1)}, bf16[3840,128]{1,0:T(8,128)(2,1)}, bf16[3840,128]{1,0:T(8,128)(2,1)}) custom-call(s32[1]{0:T(128)} %bitcast.core_ref, s32[1,15]{1,0:T(1,128)} %bitcast.6, s32[1,15]{1,0:T(1,128)S(1)} %bitcast.4, bf16[1920,512]{1,0:T(8,128)(2,1)} %lat0_hbm.1, ...), custom_call_target="tpu_custom_call" | custom-call | flops 2013265920 | bytes 7864320 | tf_op jit(solution)/shard_map/project/pallas_call | solution.py:214
  17.6 0.0 copy-start.2
  17.6 0.0 copy-start
  17.6 0.0 copy-start.1
  17.6 2.3 %all-to-all-done.q_ref = bf16[16,64,128]{2,1,0:T(8,128)(2,1)S(1)} async-done(((bf16[16,64,128]{2,1,0:T(8,128)(2,1)}), bf16[16,64,128]{2,1,0:T(8,128)(2,1)S(1)}, u32[]{:S(2)}, u32[]{:S(2)}) %all-to-all-start) | async-done | bytes 262176 | tf_op jit(solution)/shard_map/all_to_all | solution.py:511
  19.8 7.2 %attend.1 = bf16[16,72,128]{2,1,0:T(8,128)(2,1)} custom-call(bf16[16,64,128]{2,1,0:T(8,128)(2,1)S(1)} %all-to-all-done.q_ref, bf16[3840,128]{1,0:T(8,128)(2,1)S(1)} %get-tuple-element.16.k0_ref, bf16[3840,128]{1,0:T(8,128)(2,1)} %get-tuple-element.17.v0_hbm, bf16[3840,128]{1,0:T(8,128)(2,1)} %get-tuple-element.18.k_hbm, ...), custom_call_target="tpu_custom_call" | custom-call | flops 2013265920 | bytes 3932160 | tf_op jit(solution)/shard_map/attend/pallas_call | solution.py:332
  27.1 3.7 %all-to-all-start.1 = ((bf16[16,72,128]{2,1,0:T(8,128)(2,1)}), bf16[16,72,128]{2,1,0:T(8,128)(2,1)S(1)}, u32[]{:S(2)}, u32[]{:S(2)}) async-start(bf16[16,72,128]{2,1,0:T(8,128)(2,1)} %attend.1), calls=%async_computation.1 | async-start | bytes 589824 | tf_op jit(solution)/shard_map/all_to_all | solution.py:514
  30.7 0.0 copy-done.2
  30.8 0.0 copy-done
  30.8 0.0 copy-done.1
  30.8 6.2 %suffix.1 = (f32[128,128]{1,0:T(8,128)S(1)}, f32[128,128]{1,0:T(8,128)S(1)}, f32[128,128]{1,0:T(8,128)S(1)}) custom-call(s32[1]{0:T(128)S(6)} %copy.15.len_ref, bf16[128,128]{1,0:T(8,128)(2,1)S(1)} %copy-done, bf16[16,512]{1,0:T(8,128)(2,1)S(1)} %copy-done.1, bf16[16,512]{1,0:T(8,128)(2,1)S(1)} %pad.4.nv_ref, bf16[1,4096,512]{2,1,0:T(8,128)(2,1)} %k_ref.1, ...), custom_call_target="tpu_custom_call" | custom-call | flops 268435456 | bytes 8388608 | tf_op jit(solution)/shard_map/suffix/pallas_call | solution.py:423
  37.0 4.4 %all-to-all-done.1.got_ref = bf16[16,72,128]{2,1,0:T(8,128)(2,1)S(1)} async-done(((bf16[16,72,128]{2,1,0:T(8,128)(2,1)}), bf16[16,72,128]{2,1,0:T(8,128)(2,1)S(1)}, u32[]{:S(2)}, u32[]{:S(2)}) %all-to-all-start.1) | async-done | bytes 294944 | tf_op jit(solution)/shard_map/all_to_all | solution.py:514
  41.3 0.9 %combine.1 = bf16[1,4,4096]{2,1,0:T(4,128)(2,1)} custom-call(bf16[16,72,128]{2,1,0:T(8,128)(2,1)S(1)} %all-to-all-done.1.got_ref, f32[128,128]{1,0:T(8,128)S(1)} %get-tuple-element.22.acc_ref, f32[128,128]{1,0:T(8,128)S(1)} %get-tuple-element.23.peak_ref, f32[128,128]{1,0:T(8,128)S(1)} %get-tuple-element.24.total_ref), custom_call_target="tpu_custom_call" | custom-call | tf_op jit(solution)/shard_map/combine/pallas_call | solution.py:482
  (1 shorter events, 0.0 us)
Async XLA Ops:
  0.0 11.2 %collective-permute-start.1 = (bf16[1920,512]{1,0:T(8,128)(2,1)}, bf16[1920,512]{1,0:T(8,128)(2,1)S(1)}, u32[]{:S(2)}, u32[]{:S(2)}) collective-permute-start(bf16[1920,512]{1,0:T(8,128)(2,1)} %lat0_hbm.1), channel_id=1, source_target_pairs={{0,1},{1,0},{2,3},{3,2},{4,5},{5,4},{6,7},{7,6},{8,9},{9,8},{10,11... | collective-permute-start | bytes 5898248 | tf_op jit(solution)/shard_map/ppermute | solution.py:509
  2.7 17.1 %all-to-all-start = ((bf16[16,64,128]{2,1,0:T(8,128)(2,1)}), bf16[16,64,128]{2,1,0:T(8,128)(2,1)S(1)}, u32[]{:S(2)}, u32[]{:S(2)}) async-start(bf16[16,64,128]{2,1,0:T(8,128)(2,1)} %get-tuple-element.15), calls=%async_computation | async-start | bytes 524288 | tf_op jit(solution)/shard_map/all_to_all | solution.py:511
  9.8 1.4 %collective-permute-start = (s32[15]{0:T(128)}, s32[15]{0:T(128)S(1)}, u32[]{:S(2)}, u32[]{:S(2)}) collective-permute-start(s32[15]{0:T(128)} %param.15), channel_id=1, source_target_pairs={{0,1},{1,0},{2,3},{3,2},{4,5},{5,4},{6,7},{7,6},{8,9},{9,8},{10,11... | collective-permute-start | bytes 188 | tf_op jit(solution)/shard_map/ppermute | solution.py:510
  17.6 13.2 %copy-start.2 = (bf16[1,4,512]{2,1,0:T(4,128)(2,1)S(1)}, bf16[1,4,512]{2,1,0:T(4,128)(2,1)}, u32[]{:S(2)}) copy-start(bf16[1,4,512]{2,1,0:T(4,128)(2,1)} %param.20) | copy-start | bytes 12292
  17.6 13.2 %copy-start = (bf16[128,128]{1,0:T(8,128)(2,1)S(1)}, bf16[128,128]{1,0:T(8,128)(2,1)}, u32[]{:S(2)}) copy-start(bf16[128,128]{1,0:T(8,128)(2,1)} %get-tuple-element.20.q_ref) | copy-start | bytes 98308
  17.6 13.2 %copy-start.1 = (bf16[16,512]{1,0:T(8,128)(2,1)S(1)}, bf16[16,512]{1,0:T(8,128)(2,1)}, u32[]{:S(2)}) copy-start(bf16[16,512]{1,0:T(8,128)(2,1)} %get-tuple-element.21.nk_ref) | copy-start | bytes 49156
  27.1 14.2 %all-to-all-start.1 = ((bf16[16,72,128]{2,1,0:T(8,128)(2,1)}), bf16[16,72,128]{2,1,0:T(8,128)(2,1)S(1)}, u32[]{:S(2)}, u32[]{:S(2)}) async-start(bf16[16,72,128]{2,1,0:T(8,128)(2,1)} %attend.1), calls=%async_computation.1 | async-start | bytes 589824 | tf_op jit(solution)/shard_map/all_to_all | solution.py:514

commit v4 on v3

--- a/solution.py
+++ b/solution.py
@@ -489,6 +489,17 @@
     )(got, acc, peak, total)
 
 
+def exchange_order(count):
+    chips = count // 2
+    middle = chips // 2 / 2 - 0.4
+    order = sorted(range(chips), key=lambda chip: (1 - chip % 2, abs(chip // 2 - middle)))
+    return [[2 * chip + side for chip in order for side in range(2)]]
+
+
+def exchange(x, order):
+    return lax.all_to_all(x, "seq", split_axis=0, concat_axis=0, tiled=True, axis_index_groups=order)
+
+
 def local(
     prefix_latent,
     block_order,
@@ -508,10 +519,11 @@
     send, own, new_rot = rotate_queries(queries, new_keys, suffix_len, prefix, count)
     other_latent = lax.ppermute(prefix_latent, "seq", swap)
     other_order = lax.ppermute(block_order, "seq", swap)
-    gathered = lax.all_to_all(send, "seq", split_axis=0, concat_axis=0, tiled=True)
+    order = exchange_order(count)
+    gathered = exchange(send, order)
     projected = project(core, block_order, other_order, prefix_latent, other_latent, key_up, value_up)
     parts = attend(gathered, *projected)
-    got = lax.all_to_all(parts, "seq", split_axis=0, concat_axis=0, tiled=True)
+    got = exchange(parts, order)
     new_pad = jnp.pad(new_values[0], ((0, 16 - STEPS), (0, 0)))
     acc, peak, total = suffix(suffix_len, own, new_rot, new_pad, suffix_keys, suffix_values)
     return combine(got, acc, peak, total)

time: 42.7 us -> 39.5 us (0.925)
  Pallas kernels: 22.3 us -> 19 us
  starting transfers between devices: 11.6 us -> 13.7 us
  waiting for transfers between devices: 7.57 us -> 5.57 us
    pallas_call x1, Pallas kernels: 6.17 us -> 2.9 us  [suffix(): pl.pallas_call(suffix_kernel, out_shape=(out, out, out), grid_spec=pltpu....]
    all_to_all x2, starting transfers between devices: 10.7 us -> 13.1 us  [exchange(): lax.all_to_all(x, 'seq', split_axis=0, concat_axis=0, tiled=True, axis_in...]
    all_to_all x2, waiting for transfers between devices: 6.61 us -> 4.46 us  [exchange(): lax.all_to_all(x, 'seq', split_axis=0, concat_axis=0, tiled=True, axis_in...]
  transfers between devices with their start and end apart: 4 -> 4, of which waited for: 3 -> 2; matrix products, arithmetic and copies ran while one was open for 0% -> 0% of each run, Pallas kernels for 34% -> 28%
where the time goes in v4:
time: 39.5 us; the launch traced here: 39 us
  Pallas kernels  19 us (48%)
  starting transfers between devices  13.7 us (35%)
  waiting for transfers between devices  5.57 us (14%)
  between operations  0.74 us (2%)
    all_to_all x2, starting transfers between devices, exchange(): lax.all_to_all(x, 'seq', split_axis=0, concat_axis=0, tiled=True, axis_in...  13.1 us
    pallas_call x1, Pallas kernels, attend(): pl.pallas_call(functools.partial(attend_kernel, math.gcd(count, Q_GROUP))...  7.22 us
    pallas_call x1, Pallas kernels, project(): pl.pallas_call(project_kernel, out_shape=(out, out_far, out_far, out_far)...  6.36 us
    all_to_all x2, waiting for transfers between devices, exchange(): lax.all_to_all(x, 'seq', split_axis=0, concat_axis=0, tiled=True, axis_in...  4.46 us
    pallas_call x1, Pallas kernels, suffix(): pl.pallas_call(suffix_kernel, out_shape=(out, out, out), grid_spec=pltpu....  2.9 us
    pallas_call x1, Pallas kernels, rotate_queries(): pl.pallas_call(functools.partial(query_kernel, prefix, count), out_shape=...  1.64 us
    ppermute x1, waiting for transfers between devices, local(): other_order = lax.ppermute(block_order, 'seq', swap)  1.11 us
    pallas_call x1, Pallas kernels, combine(): pl.pallas_call(combine_kernel, out_shape=jax.ShapeDtypeStruct((1, STEPS,...  0.89 us
  transfers between devices with their start and end apart: 4, of which 2 were waited for; matrix products, arithmetic and copies ran while one was open for 0% of the time, Pallas kernels for 28%

profile of v4, /device:TPU:0, one launch (start us, length us, event | category | flops | bytes accessed | tf_op | source)
XLA Modules:
  0.0 39.0 jit_solution(18029718807060115640)
XLA Ops:
  0.0 0.5 %collective-permute-start.1 = (bf16[1920,512]{1,0:T(8,128)(2,1)}, bf16[1920,512]{1,0:T(8,128)(2,1)S(1)}, u32[]{:S(2)}, u32[]{:S(2)}) collective-permute-start(bf16[1920,512]{1,0:T(8,128)(2,1)} %lat0_hbm.1), channel_id=1, source_target_pairs={{0,1},{1,0},{2,3},{3,2},{4,5},{5,4},{6,7},{7,6},{8,9},{9,8},{10,11... | collective-permute-start | bytes 5898248 | tf_op jit(solution)/shard_map/ppermute | solution.py:520
  1.1 1.6 %rotate_queries.1 = (bf16[16,64,128]{2,1,0:T(8,128)(2,1)}, bf16[128,128]{1,0:T(8,128)(2,1)}, bf16[16,512]{1,0:T(8,128)(2,1)}) custom-call(s32[1]{0:T(128)S(6)} %copy.15.len_ref, s32[8,128]{1,0:T(8,128)} %constant.26.clone.table_ref, bf16[1,4,4096]{2,1,0:T(4,128)(2,1)} %q_ref.1, bf16[1,4,512]{2,1,0:T(4,128)(2,1)} %nk_ref.1), custom_call_target="tpu_custom_call" | custom-call | tf_op jit(solution)/shard_map/rotate_queries/pallas_call | solution.py:101
  2.7 8.0 %all-to-all-start = ((bf16[16,64,128]{2,1,0:T(8,128)(2,1)}), bf16[16,64,128]{2,1,0:T(8,128)(2,1)S(1)}, u32[]{:S(2)}, u32[]{:S(2)}) async-start(bf16[16,64,128]{2,1,0:T(8,128)(2,1)} %get-tuple-element.15), calls=%async_computation | async-start | bytes 524288 | tf_op jit(solution)/shard_map/all_to_all | solution.py:500
  10.7 0.1 collective-permute-start
  10.8 1.1 %collective-permute-done = s32[15]{0:T(128)S(1)} collective-permute-done((s32[15]{0:T(128)}, s32[15]{0:T(128)S(1)}, u32[]{:S(2)}, u32[]{:S(2)}) %collective-permute-start) | collective-permute-done | bytes 92 | tf_op jit(solution)/shard_map/ppermute | solution.py:521
  11.9 0.0 collective-permute-done.1.lat1_hbm
  12.0 6.4 %project.1 = (bf16[3840,128]{1,0:T(8,128)(2,1)S(1)}, bf16[3840,128]{1,0:T(8,128)(2,1)}, bf16[3840,128]{1,0:T(8,128)(2,1)}, bf16[3840,128]{1,0:T(8,128)(2,1)}) custom-call(s32[1]{0:T(128)} %bitcast.core_ref, s32[1,15]{1,0:T(1,128)} %bitcast.6, s32[1,15]{1,0:T(1,128)S(1)} %bitcast.4, bf16[1920,512]{1,0:T(8,128)(2,1)} %lat0_hbm.1, ...), custom_call_target="tpu_custom_call" | custom-call | flops 2013265920 | bytes 7864320 | tf_op jit(solution)/shard_map/project/pallas_call | solution.py:214
  18.3 0.0 copy-start.2
  18.3 0.0 copy-start
  18.3 0.0 copy-start.1
  18.4 0.0 all-to-all-done.q_ref
  18.4 7.2 %attend.1 = bf16[16,72,128]{2,1,0:T(8,128)(2,1)} custom-call(bf16[16,64,128]{2,1,0:T(8,128)(2,1)S(1)} %all-to-all-done.q_ref, bf16[3840,128]{1,0:T(8,128)(2,1)S(1)} %get-tuple-element.16.k0_ref, bf16[3840,128]{1,0:T(8,128)(2,1)} %get-tuple-element.17.v0_hbm, bf16[3840,128]{1,0:T(8,128)(2,1)} %get-tuple-element.18.k_hbm, ...), custom_call_target="tpu_custom_call" | custom-call | flops 2013265920 | bytes 3932160 | tf_op jit(solution)/shard_map/attend/pallas_call | solution.py:332
  25.6 5.1 %all-to-all-start.1 = ((bf16[16,72,128]{2,1,0:T(8,128)(2,1)}), bf16[16,72,128]{2,1,0:T(8,128)(2,1)S(1)}, u32[]{:S(2)}, u32[]{:S(2)}) async-start(bf16[16,72,128]{2,1,0:T(8,128)(2,1)} %attend.1), calls=%async_computation.1 | async-start | bytes 589824 | tf_op jit(solution)/shard_map/all_to_all | solution.py:500
  30.7 0.0 copy-done.2
  30.7 0.0 copy-done
  30.8 0.0 copy-done.1
  30.8 2.9 %suffix.1 = (f32[128,128]{1,0:T(8,128)S(1)}, f32[128,128]{1,0:T(8,128)S(1)}, f32[128,128]{1,0:T(8,128)S(1)}) custom-call(s32[1]{0:T(128)S(6)} %copy.15.len_ref, bf16[128,128]{1,0:T(8,128)(2,1)S(1)} %copy-done, bf16[16,512]{1,0:T(8,128)(2,1)S(1)} %copy-done.1, bf16[16,512]{1,0:T(8,128)(2,1)S(1)} %pad.4.nv_ref, bf16[1,4096,512]{2,1,0:T(8,128)(2,1)} %k_ref.1, ...), custom_call_target="tpu_custom_call" | custom-call | flops 268435456 | bytes 8388608 | tf_op jit(solution)/shard_map/suffix/pallas_call | solution.py:423
  33.7 4.5 %all-to-all-done.1.got_ref = bf16[16,72,128]{2,1,0:T(8,128)(2,1)S(1)} async-done(((bf16[16,72,128]{2,1,0:T(8,128)(2,1)}), bf16[16,72,128]{2,1,0:T(8,128)(2,1)S(1)}, u32[]{:S(2)}, u32[]{:S(2)}) %all-to-all-start.1) | async-done | bytes 294944 | tf_op jit(solution)/shard_map/all_to_all | solution.py:500
  38.1 0.9 %combine.1 = bf16[1,4,4096]{2,1,0:T(4,128)(2,1)} custom-call(bf16[16,72,128]{2,1,0:T(8,128)(2,1)S(1)} %all-to-all-done.1.got_ref, f32[128,128]{1,0:T(8,128)S(1)} %get-tuple-element.22.acc_ref, f32[128,128]{1,0:T(8,128)S(1)} %get-tuple-element.23.peak_ref, f32[128,128]{1,0:T(8,128)S(1)} %get-tuple-element.24.total_ref), custom_call_target="tpu_custom_call" | custom-call | tf_op jit(solution)/shard_map/combine/pallas_call | solution.py:482
  (1 shorter events, 0.0 us)
Async XLA Ops:
  0.0 12.0 %collective-permute-start.1 = (bf16[1920,512]{1,0:T(8,128)(2,1)}, bf16[1920,512]{1,0:T(8,128)(2,1)S(1)}, u32[]{:S(2)}, u32[]{:S(2)}) collective-permute-start(bf16[1920,512]{1,0:T(8,128)(2,1)} %lat0_hbm.1), channel_id=1, source_target_pairs={{0,1},{1,0},{2,3},{3,2},{4,5},{5,4},{6,7},{7,6},{8,9},{9,8},{10,11... | collective-permute-start | bytes 5898248 | tf_op jit(solution)/shard_map/ppermute | solution.py:520
  2.7 15.6 %all-to-all-start = ((bf16[16,64,128]{2,1,0:T(8,128)(2,1)}), bf16[16,64,128]{2,1,0:T(8,128)(2,1)S(1)}, u32[]{:S(2)}, u32[]{:S(2)}) async-start(bf16[16,64,128]{2,1,0:T(8,128)(2,1)} %get-tuple-element.15), calls=%async_computation | async-start | bytes 524288 | tf_op jit(solution)/shard_map/all_to_all | solution.py:500
  10.7 1.3 %collective-permute-start = (s32[15]{0:T(128)}, s32[15]{0:T(128)S(1)}, u32[]{:S(2)}, u32[]{:S(2)}) collective-permute-start(s32[15]{0:T(128)} %param.15), channel_id=1, source_target_pairs={{0,1},{1,0},{2,3},{3,2},{4,5},{5,4},{6,7},{7,6},{8,9},{9,8},{10,11... | collective-permute-start | bytes 188 | tf_op jit(solution)/shard_map/ppermute | solution.py:521
  18.3 12.4 %copy-start.2 = (bf16[1,4,512]{2,1,0:T(4,128)(2,1)S(1)}, bf16[1,4,512]{2,1,0:T(4,128)(2,1)}, u32[]{:S(2)}) copy-start(bf16[1,4,512]{2,1,0:T(4,128)(2,1)} %param.20) | copy-start | bytes 12292
  18.3 12.4 %copy-start = (bf16[128,128]{1,0:T(8,128)(2,1)S(1)}, bf16[128,128]{1,0:T(8,128)(2,1)}, u32[]{:S(2)}) copy-start(bf16[128,128]{1,0:T(8,128)(2,1)} %get-tuple-element.20.q_ref) | copy-start | bytes 98308
  18.3 12.4 %copy-start.1 = (bf16[16,512]{1,0:T(8,128)(2,1)S(1)}, bf16[16,512]{1,0:T(8,128)(2,1)}, u32[]{:S(2)}) copy-start(bf16[16,512]{1,0:T(8,128)(2,1)} %get-tuple-element.21.nk_ref) | copy-start | bytes 49156
  25.6 12.5 %all-to-all-start.1 = ((bf16[16,72,128]{2,1,0:T(8,128)(2,1)}), bf16[16,72,128]{2,1,0:T(8,128)(2,1)S(1)}, u32[]{:S(2)}, u32[]{:S(2)}) async-start(bf16[16,72,128]{2,1,0:T(8,128)(2,1)} %attend.1), calls=%async_computation.1 | async-start | bytes 589824 | tf_op jit(solution)/shard_map/all_to_all | solution.py:500

commit v5 on v4

--- a/solution.py
+++ b/solution.py
@@ -29,6 +29,8 @@
 PER = 15
 Q_GROUP = 16
 CHUNKS = 5
+NEAR = 1
+LATE = 3
 F32 = jnp.float32
 BF16 = jnp.bfloat16
 
@@ -124,6 +126,7 @@
     rc_ref,
     rs_ref,
     k0_ref,
+    v0_ref,
     v0_hbm,
     k_hbm,
     v_hbm,
@@ -131,7 +134,7 @@
     bs_ref,
     lat_ref,
     w_ref,
-    v0_ref,
+    rest_ref,
     k_ref,
     v_ref,
     in_sem,
@@ -179,8 +182,16 @@
         lat = lat_ref[at, :]
         keys = jnp.dot(lat, w_ref[...], preferred_element_type=F32)
         values = keys[:, WIDE:].astype(BF16)
-        for target, k in ((v0_ref, 0), (v_ref, 1)):
-            target[at, :] = values[:, k * HD : (k + 1) * HD]
+        v_ref[at, :] = values[:, HD:]
+        low, high = slot * size, (slot + 1) * size
+        split = min(max(v0_ref.shape[0], low), high)
+        if low < split:
+            v0_ref[low:split, :] = values[: split - low, :HD]
+        moves = [(k_ref.at[at], k_hbm.at[at]), (v_ref.at[at], v_hbm.at[at])]
+        if split < high:
+            rest = pl.ds(split - v0_ref.shape[0], high - split)
+            rest_ref[rest, :] = values[split - low :, :HD]
+            moves.append((rest_ref.at[rest], v0_hbm.at[rest]))
         for i in range(per):
             b = slot * per + i
             block_cos = bc_ref[b : b + 1, :]
@@ -190,8 +201,8 @@
             for target, k in ((k0_ref, 0), (k_ref, 1)):
                 part = keys[i * BLK : (i + 1) * BLK, k * HD : (k + 1) * HD]
                 target[b * BLK : (b + 1) * BLK, :] = turn(part, cosine, sine).astype(BF16)
-        for kind, (source, target) in enumerate(((v0_ref, v0_hbm), (k_ref, k_hbm), (v_ref, v_hbm))):
-            store = pltpu.make_async_copy(source.at[at], target.at[at], out_sem.at[slot * 3 + kind])
+        for kind, (source, target) in enumerate(moves):
+            store = pltpu.make_async_copy(source, target, out_sem.at[slot * 3 + kind])
             store.start()
             stores.append(store)
     for store in stores:
@@ -211,17 +222,18 @@
     pad = -(-2 * blocks // 8) * 8
     out = jax.ShapeDtypeStruct((rows, HD), BF16)
     out_far = pltpu.HBM((rows, HD), BF16)
+    close = rows // CHUNKS * NEAR
     return pl.pallas_call(
         project_kernel,
-        out_shape=(out, out_far, out_far, out_far),
+        out_shape=(out, jax.ShapeDtypeStruct((close, HD), BF16), pltpu.HBM((rows - close, HD), BF16), out_far, out_far),
         in_specs=[smem, vmem, vmem, hbm, hbm, hbm, hbm, vmem, vmem, vmem],
-        out_specs=(vmem, hbm, hbm, hbm),
+        out_specs=(vmem, vmem, hbm, hbm, hbm),
         scratch_shapes=[
             pltpu.VMEM((pad, HD), F32),
             pltpu.VMEM((pad, HD), F32),
             pltpu.VMEM((rows, rank), BF16),
             pltpu.VMEM((rank, 2 * WIDE), BF16),
-            pltpu.VMEM((rows, HD), BF16),
+            pltpu.VMEM((rows - close, HD), BF16),
             pltpu.VMEM((rows, HD), BF16),
             pltpu.VMEM((rows, HD), BF16),
             pltpu.SemaphoreType.DMA((slots,)),
@@ -258,13 +270,13 @@
     return first, second, rest - second
 
 
-def attend_kernel(per, q_ref, k0_ref, v0_hbm, k_hbm, v_hbm, out_ref, v0_ref, k_ref, v_ref, stat_ref, sem):
+def attend_kernel(per, q_ref, k0_ref, v0_ref, v0_hbm, k_hbm, v_hbm, out_ref, rest_ref, k_ref, v_ref, stat_ref, sem):
     nt = (((1,), (1,)), ((), ()))
     row = lax.broadcasted_iota(jnp.int32, (KROWS, HD), 0)
     lane = lax.broadcasted_iota(jnp.int32, (KROWS, HD), 1)
     place = lax.broadcasted_iota(jnp.int32, (8, HD), 0)
     fetches = [
-        pltpu.make_async_copy(v0_hbm, v0_ref, sem.at[0]),
+        pltpu.make_async_copy(v0_hbm, rest_ref, sem.at[0]),
         pltpu.make_async_copy(k_hbm, k_ref, sem.at[1]),
         pltpu.make_async_copy(v_hbm, v_ref, sem.at[2]),
     ]
@@ -272,12 +284,12 @@
         fetch.start()
 
     for k in range(HALF_KV):
-        if k:
+        if k and LATE < 0:
             fetches[1].wait()
             fetches[2].wait()
-        keys, values = ((k0_ref, v0_ref), (k_ref, v_ref))[k]
-
-        def group(g, first=False, k=k, keys=keys, values=values):
+        keys = (k0_ref, k_ref)[k]
+
+        def group(g, first=False, k=k, keys=keys):
             base = g * per
             rows = slice(k * KROWS, (k + 1) * KROWS)
             q = q_ref[pl.ds(base, per), rows, :].reshape(per * KROWS, HD)
@@ -292,14 +304,23 @@
                 if c + 1 < CHUNKS:
                     ahead = score(c + 1)
                 best = jnp.max(s, -1, keepdims=True)
-                if first and c == 0:
+                if first and c == NEAR:
                     fetches[0].wait()
+                if first and c == LATE:
+                    fetches[1].wait()
+                    fetches[2].wait()
                 if c:
                     best = jnp.maximum(peak, best)
                     keep = jnp.exp2((peak - best) * EXP2)
                 e = jnp.exp2((s - best) * EXP2)
                 here = jnp.sum(e, -1, keepdims=True)
-                o = jnp.dot(e.astype(BF16), values[c * width : (c + 1) * width, :], preferred_element_type=F32)
+                if k:
+                    values = v_ref[c * width : (c + 1) * width, :]
+                elif c < NEAR:
+                    values = v0_ref[c * width : (c + 1) * width, :]
+                else:
+                    values = rest_ref[(c - NEAR) * width : (c - NEAR + 1) * width, :]
+                o = jnp.dot(e.astype(BF16), values, preferred_element_type=F32)
                 total = total * keep + here if c else here
                 acc = acc * keep + o if c else o
                 peak = best
@@ -324,7 +345,7 @@
             pl.loop(1, groups)(group)
 
 
-def attend(q, k0, v0, k1, v1):
+def attend(q, k0, v0, rest, k1, v1):
     count = q.shape[0]
     rows = k0.shape[0]
     vmem = pl.BlockSpec(memory_space=pltpu.VMEM)
@@ -332,10 +353,10 @@
     return pl.pallas_call(
         functools.partial(attend_kernel, math.gcd(count, Q_GROUP)),
         out_shape=jax.ShapeDtypeStruct((count, PAY, HD), BF16),
-        in_specs=[vmem, vmem, hbm, hbm, hbm],
+        in_specs=[vmem, vmem, vmem, hbm, hbm, hbm],
         out_specs=vmem,
         scratch_shapes=[
-            pltpu.VMEM((rows, HD), BF16),
+            pltpu.VMEM(rest.shape, BF16),
             pltpu.VMEM((rows, HD), BF16),
             pltpu.VMEM((rows, HD), BF16),
             pltpu.VMEM((count, 8, HD), F32),
@@ -348,7 +369,7 @@
             transcendentals=count * HROWS * rows,
         ),
         name="attend",
-    )(q, k0, far(v0), far(k1), far(v1))
+    )(q, k0, v0, far(rest), far(k1), far(v1))
 
 
 def suffix_kernel(len_ref, q_ref, nk_ref, nv_ref, k_ref, v_ref, acc_ref, peak_ref, total_ref):

time: 39.5 us -> 39.1 us (0.990)
  waiting for transfers between devices: 5.57 us -> 3.28 us
  Pallas kernels: 19 us -> 20.8 us
    pallas_call x1, Pallas kernels: 2.9 us -> 5.19 us  [suffix(): pl.pallas_call(suffix_kernel, out_shape=(out, out, out), grid_spec=pltpu....]
    all_to_all x2, waiting for transfers between devices: 4.46 us -> 2.17 us  [exchange(): lax.all_to_all(x, 'seq', split_axis=0, concat_axis=0, tiled=True, axis_in...]
    pallas_call x1, Pallas kernels: 7.22 us -> 6.72 us  [attend(): pl.pallas_call(functools.partial(attend_kernel, math.gcd(count, Q_GROUP))...]
  transfers between devices with their start and end apart: 4 -> 4, of which waited for: 2 -> 2; matrix products, arithmetic and copies ran while one was open for 0% -> 0% of each run, Pallas kernels for 28% -> 34%
where the time goes in v5:
time: 39.1 us; the launch traced here: 38.6 us
  Pallas kernels  20.8 us (53%)
  starting transfers between devices  13.7 us (35%)
  waiting for transfers between devices  3.28 us (8%)
  between operations  0.74 us (2%)
    all_to_all x2, starting transfers between devices, exchange(): lax.all_to_all(x, 'seq', split_axis=0, concat_axis=0, tiled=True, axis_in...  13.1 us
    pallas_call x1, Pallas kernels, attend(): pl.pallas_call(functools.partial(attend_kernel, math.gcd(count, Q_GROUP))...  6.72 us
    pallas_call x1, Pallas kernels, project(): pl.pallas_call(project_kernel, out_shape=(out, jax.ShapeDtypeStruct((clos...  6.4 us
    pallas_call x1, Pallas kernels, suffix(): pl.pallas_call(suffix_kernel, out_shape=(out, out, out), grid_spec=pltpu....  5.19 us
    all_to_all x2, waiting for transfers between devices, exchange(): lax.all_to_all(x, 'seq', split_axis=0, concat_axis=0, tiled=True, axis_in...  2.17 us
    pallas_call x1, Pallas kernels, rotate_queries(): pl.pallas_call(functools.partial(query_kernel, prefix, count), out_shape=...  1.64 us
    ppermute x1, waiting for transfers between devices, local(): other_order = lax.ppermute(block_order, 'seq', swap)  1.11 us
    pallas_call x1, Pallas kernels, combine(): pl.pallas_call(combine_kernel, out_shape=jax.ShapeDtypeStruct((1, STEPS,...  0.89 us
  transfers between devices with their start and end apart: 4, of which 2 were waited for; matrix products, arithmetic and copies ran while one was open for 0% of the time, Pallas kernels for 34%

profile of v5, /device:TPU:0, one launch (start us, length us, event | category | flops | bytes accessed | tf_op | source)
XLA Modules:
  0.0 38.6 jit_solution(9725461623951101522)
XLA Ops:
  0.0 0.5 %collective-permute-start.1 = (bf16[1920,512]{1,0:T(8,128)(2,1)}, bf16[1920,512]{1,0:T(8,128)(2,1)S(1)}, u32[]{:S(2)}, u32[]{:S(2)}) collective-permute-start(bf16[1920,512]{1,0:T(8,128)(2,1)} %lat0_hbm.1), channel_id=1, source_target_pairs={{0,1},{1,0},{2,3},{3,2},{4,5},{5,4},{6,7},{7,6},{8,9},{9,8},{10,11... | collective-permute-start | bytes 5898248 | tf_op jit(solution)/shard_map/ppermute | solution.py:541
  1.1 1.6 %rotate_queries.1 = (bf16[16,64,128]{2,1,0:T(8,128)(2,1)}, bf16[128,128]{1,0:T(8,128)(2,1)}, bf16[16,512]{1,0:T(8,128)(2,1)}) custom-call(s32[1]{0:T(128)S(6)} %copy.15.len_ref, s32[8,128]{1,0:T(8,128)} %constant.26.clone.table_ref, bf16[1,4,4096]{2,1,0:T(4,128)(2,1)} %q_ref.1, bf16[1,4,512]{2,1,0:T(4,128)(2,1)} %nk_ref.1), custom_call_target="tpu_custom_call" | custom-call | tf_op jit(solution)/shard_map/rotate_queries/pallas_call | solution.py:103
  2.7 8.0 %all-to-all-start = ((bf16[16,64,128]{2,1,0:T(8,128)(2,1)}), bf16[16,64,128]{2,1,0:T(8,128)(2,1)S(1)}, u32[]{:S(2)}, u32[]{:S(2)}) async-start(bf16[16,64,128]{2,1,0:T(8,128)(2,1)} %get-tuple-element.16), calls=%async_computation | async-start | bytes 524288 | tf_op jit(solution)/shard_map/all_to_all | solution.py:521
  10.7 0.1 collective-permute-start
  10.8 1.1 %collective-permute-done = s32[15]{0:T(128)S(1)} collective-permute-done((s32[15]{0:T(128)}, s32[15]{0:T(128)S(1)}, u32[]{:S(2)}, u32[]{:S(2)}) %collective-permute-start) | collective-permute-done | bytes 92 | tf_op jit(solution)/shard_map/ppermute | solution.py:542
  12.0 0.0 collective-permute-done.1.lat1_hbm
  12.0 6.4 %project.1 = (bf16[3840,128]{1,0:T(8,128)(2,1)S(1)}, bf16[768,128]{1,0:T(8,128)(2,1)S(1)}, bf16[3072,128]{1,0:T(8,128)(2,1)}, bf16[3840,128]{1,0:T(8,128)(2,1)}, bf16[3840,128]{1,0:T(8,128)(2,1)}) custom-call(s32[1]{0:T(128)} %bitcast.core_ref, s32[1,15]{1,0:T(1,128)} %bitcast.6, s32[1,15]{1,0:T(1,128)S(1)} %bitcast.4, bf16[1920,512]{1,0:T(8,128)(2,1)} %lat0_hbm.1, ...), custom_call_target="tpu_custom_call" | custom-call | flops 2013265920 | bytes 7864320 | tf_op jit(solution)/shard_map/project/pallas_call | solution.py:226
  18.4 0.0 copy-start.2
  18.4 0.0 copy-start
  18.4 0.0 copy-start.1
  18.4 0.0 all-to-all-done.q_ref
  18.4 6.7 %attend.1 = bf16[16,72,128]{2,1,0:T(8,128)(2,1)} custom-call(bf16[16,64,128]{2,1,0:T(8,128)(2,1)S(1)} %all-to-all-done.q_ref, bf16[3840,128]{1,0:T(8,128)(2,1)S(1)} %get-tuple-element.17.k0_ref, bf16[768,128]{1,0:T(8,128)(2,1)S(1)} %get-tuple-element.18.v0_ref, bf16[3072,128]{1,0:T(8,128)(2,1)} %get-tuple-element.19.v0_hbm, ...), custom_call_target="tpu_custom_call" | custom-call | flops 2013265920 | bytes 3932160 | tf_op jit(solution)/shard_map/attend/pallas_call | solution.py:353
  25.1 5.1 %all-to-all-start.1 = ((bf16[16,72,128]{2,1,0:T(8,128)(2,1)}), bf16[16,72,128]{2,1,0:T(8,128)(2,1)S(1)}, u32[]{:S(2)}, u32[]{:S(2)}) async-start(bf16[16,72,128]{2,1,0:T(8,128)(2,1)} %attend.1), calls=%async_computation.1 | async-start | bytes 589824 | tf_op jit(solution)/shard_map/all_to_all | solution.py:521
  30.3 0.0 copy-done.2
  30.3 0.0 copy-done
  30.3 0.0 copy-done.1
  30.3 5.2 %suffix.1 = (f32[128,128]{1,0:T(8,128)S(1)}, f32[128,128]{1,0:T(8,128)S(1)}, f32[128,128]{1,0:T(8,128)S(1)}) custom-call(s32[1]{0:T(128)S(6)} %copy.15.len_ref, bf16[128,128]{1,0:T(8,128)(2,1)S(1)} %copy-done, bf16[16,512]{1,0:T(8,128)(2,1)S(1)} %copy-done.1, bf16[16,512]{1,0:T(8,128)(2,1)S(1)} %pad.4.nv_ref, bf16[1,4096,512]{2,1,0:T(8,128)(2,1)} %k_ref.1, ...), custom_call_target="tpu_custom_call" | custom-call | flops 268435456 | bytes 8388608 | tf_op jit(solution)/shard_map/suffix/pallas_call | solution.py:444
  35.5 2.2 %all-to-all-done.1.got_ref = bf16[16,72,128]{2,1,0:T(8,128)(2,1)S(1)} async-done(((bf16[16,72,128]{2,1,0:T(8,128)(2,1)}), bf16[16,72,128]{2,1,0:T(8,128)(2,1)S(1)}, u32[]{:S(2)}, u32[]{:S(2)}) %all-to-all-start.1) | async-done | bytes 294944 | tf_op jit(solution)/shard_map/all_to_all | solution.py:521
  37.7 0.9 %combine.1 = bf16[1,4,4096]{2,1,0:T(4,128)(2,1)} custom-call(bf16[16,72,128]{2,1,0:T(8,128)(2,1)S(1)} %all-to-all-done.1.got_ref, f32[128,128]{1,0:T(8,128)S(1)} %get-tuple-element.24.acc_ref, f32[128,128]{1,0:T(8,128)S(1)} %get-tuple-element.25.peak_ref, f32[128,128]{1,0:T(8,128)S(1)} %get-tuple-element.26.total_ref), custom_call_target="tpu_custom_call" | custom-call | tf_op jit(solution)/shard_map/combine/pallas_call | solution.py:503
  (1 shorter events, 0.0 us)
Async XLA Ops:
  0.0 12.0 %collective-permute-start.1 = (bf16[1920,512]{1,0:T(8,128)(2,1)}, bf16[1920,512]{1,0:T(8,128)(2,1)S(1)}, u32[]{:S(2)}, u32[]{:S(2)}) collective-permute-start(bf16[1920,512]{1,0:T(8,128)(2,1)} %lat0_hbm.1), channel_id=1, source_target_pairs={{0,1},{1,0},{2,3},{3,2},{4,5},{5,4},{6,7},{7,6},{8,9},{9,8},{10,11... | collective-permute-start | bytes 5898248 | tf_op jit(solution)/shard_map/ppermute | solution.py:541
  2.7 15.7 %all-to-all-start = ((bf16[16,64,128]{2,1,0:T(8,128)(2,1)}), bf16[16,64,128]{2,1,0:T(8,128)(2,1)S(1)}, u32[]{:S(2)}, u32[]{:S(2)}) async-start(bf16[16,64,128]{2,1,0:T(8,128)(2,1)} %get-tuple-element.16), calls=%async_computation | async-start | bytes 524288 | tf_op jit(solution)/shard_map/all_to_all | solution.py:521
  10.7 1.3 %collective-permute-start = (s32[15]{0:T(128)}, s32[15]{0:T(128)S(1)}, u32[]{:S(2)}, u32[]{:S(2)}) collective-permute-start(s32[15]{0:T(128)} %param.15), channel_id=1, source_target_pairs={{0,1},{1,0},{2,3},{3,2},{4,5},{5,4},{6,7},{7,6},{8,9},{9,8},{10,11... | collective-permute-start | bytes 188 | tf_op jit(solution)/shard_map/ppermute | solution.py:542
  18.4 11.9 %copy-start.2 = (bf16[1,4,512]{2,1,0:T(4,128)(2,1)S(1)}, bf16[1,4,512]{2,1,0:T(4,128)(2,1)}, u32[]{:S(2)}) copy-start(bf16[1,4,512]{2,1,0:T(4,128)(2,1)} %param.20) | copy-start | bytes 12292
  18.4 11.9 %copy-start = (bf16[128,128]{1,0:T(8,128)(2,1)S(1)}, bf16[128,128]{1,0:T(8,128)(2,1)}, u32[]{:S(2)}) copy-start(bf16[128,128]{1,0:T(8,128)(2,1)} %get-tuple-element.22.q_ref) | copy-start | bytes 98308
  18.4 11.9 %copy-start.1 = (bf16[16,512]{1,0:T(8,128)(2,1)S(1)}, bf16[16,512]{1,0:T(8,128)(2,1)}, u32[]{:S(2)}) copy-start(bf16[16,512]{1,0:T(8,128)(2,1)} %get-tuple-element.23.nk_ref) | copy-start | bytes 49156
  25.1 12.5 %all-to-all-start.1 = ((bf16[16,72,128]{2,1,0:T(8,128)(2,1)}), bf16[16,72,128]{2,1,0:T(8,128)(2,1)S(1)}, u32[]{:S(2)}, u32[]{:S(2)}) async-start(bf16[16,72,128]{2,1,0:T(8,128)(2,1)} %attend.1), calls=%async_computation.1 | async-start | bytes 589824 | tf_op jit(solution)/shard_map/all_to_all | solution.py:521

commit v6 on v5

--- a/solution.py
+++ b/solution.py
@@ -30,7 +30,7 @@
 Q_GROUP = 16
 CHUNKS = 5
 NEAR = 1
-LATE = 3
+LATE = 2
 F32 = jnp.float32
 BF16 = jnp.bfloat16
 
@@ -512,8 +512,13 @@
 
 def exchange_order(count):
     chips = count // 2
-    middle = chips // 2 / 2 - 0.4
-    order = sorted(range(chips), key=lambda chip: (1 - chip % 2, abs(chip // 2 - middle)))
+    middle = chips // 2 / 2
+
+    def rank(chip):
+        side = chip % 2
+        return 1 - side, abs(chip // 2 - (middle + (-0.4 if side else 0.4)))
+
+    order = sorted(range(chips), key=rank)
     return [[2 * chip + side for chip in order for side in range(2)]]
 
 

time: 39.1 us -> 38.6 us (0.987)
  waiting for transfers between devices: 3.28 us -> 1.76 us
  Pallas kernels: 20.8 us -> 21.7 us
    all_to_all x2, waiting for transfers between devices: 2.17 us -> 0.65 us  [exchange(): lax.all_to_all(x, 'seq', split_axis=0, concat_axis=0, tiled=True, axis_in...]
    pallas_call x1, Pallas kernels: 5.19 us -> 6.16 us  [suffix(): pl.pallas_call(suffix_kernel, out_shape=(out, out, out), grid_spec=pltpu....]
  transfers between devices with their start and end apart: 4 -> 4, of which waited for: 2 -> 2; matrix products, arithmetic and copies ran while one was open for 0% -> 0% of each run, Pallas kernels for 34% -> 37%
where the time goes in v6:
time: 38.6 us; the launch traced here: 37.9 us
  Pallas kernels  21.7 us (56%)
  starting transfers between devices  13.7 us (35%)
  waiting for transfers between devices  1.76 us (5%)
  between operations  0.74 us (2%)
    all_to_all x2, starting transfers between devices, exchange(): lax.all_to_all(x, 'seq', split_axis=0, concat_axis=0, tiled=True, axis_in...  13.1 us
    pallas_call x1, Pallas kernels, attend(): pl.pallas_call(functools.partial(attend_kernel, math.gcd(count, Q_GROUP))...  6.62 us
    pallas_call x1, Pallas kernels, project(): pl.pallas_call(project_kernel, out_shape=(out, jax.ShapeDtypeStruct((clos...  6.4 us
    pallas_call x1, Pallas kernels, suffix(): pl.pallas_call(suffix_kernel, out_shape=(out, out, out), grid_spec=pltpu....  6.16 us
    pallas_call x1, Pallas kernels, rotate_queries(): pl.pallas_call(functools.partial(query_kernel, prefix, count), out_shape=...  1.64 us
    ppermute x1, waiting for transfers between devices, local(): other_order = lax.ppermute(block_order, 'seq', swap)  1.11 us
    pallas_call x1, Pallas kernels, combine(): pl.pallas_call(combine_kernel, out_shape=jax.ShapeDtypeStruct((1, STEPS,...  0.89 us
  transfers between devices with their start and end apart: 4, of which 2 were waited for; matrix products, arithmetic and copies ran while one was open for 0% of the time, Pallas kernels for 37%

profile of v6, /device:TPU:0, one launch (start us, length us, event | category | flops | bytes accessed | tf_op | source)
XLA Modules:
  0.0 37.9 jit_solution(8656246955754571040)
XLA Ops:
  0.0 0.5 %collective-permute-start.1 = (bf16[1920,512]{1,0:T(8,128)(2,1)}, bf16[1920,512]{1,0:T(8,128)(2,1)S(1)}, u32[]{:S(2)}, u32[]{:S(2)}) collective-permute-start(bf16[1920,512]{1,0:T(8,128)(2,1)} %lat0_hbm.1), channel_id=1, source_target_pairs={{0,1},{1,0},{2,3},{3,2},{4,5},{5,4},{6,7},{7,6},{8,9},{9,8},{10,11... | collective-permute-start | bytes 5898248 | tf_op jit(solution)/shard_map/ppermute | solution.py:546
  1.1 1.6 %rotate_queries.1 = (bf16[16,64,128]{2,1,0:T(8,128)(2,1)}, bf16[128,128]{1,0:T(8,128)(2,1)}, bf16[16,512]{1,0:T(8,128)(2,1)}) custom-call(s32[1]{0:T(128)S(6)} %copy.15.len_ref, s32[8,128]{1,0:T(8,128)} %constant.26.clone.table_ref, bf16[1,4,4096]{2,1,0:T(4,128)(2,1)} %q_ref.1, bf16[1,4,512]{2,1,0:T(4,128)(2,1)} %nk_ref.1), custom_call_target="tpu_custom_call" | custom-call | tf_op jit(solution)/shard_map/rotate_queries/pallas_call | solution.py:103
  2.7 8.0 %all-to-all-start = ((bf16[16,64,128]{2,1,0:T(8,128)(2,1)}), bf16[16,64,128]{2,1,0:T(8,128)(2,1)S(1)}, u32[]{:S(2)}, u32[]{:S(2)}) async-start(bf16[16,64,128]{2,1,0:T(8,128)(2,1)} %get-tuple-element.16), calls=%async_computation | async-start | bytes 524288 | tf_op jit(solution)/shard_map/all_to_all | solution.py:526
  10.7 0.1 collective-permute-start
  10.8 1.1 %collective-permute-done = s32[15]{0:T(128)S(1)} collective-permute-done((s32[15]{0:T(128)}, s32[15]{0:T(128)S(1)}, u32[]{:S(2)}, u32[]{:S(2)}) %collective-permute-start) | collective-permute-done | bytes 92 | tf_op jit(solution)/shard_map/ppermute | solution.py:547
  12.0 0.0 collective-permute-done.1.lat1_hbm
  12.0 6.4 %project.1 = (bf16[3840,128]{1,0:T(8,128)(2,1)S(1)}, bf16[768,128]{1,0:T(8,128)(2,1)S(1)}, bf16[3072,128]{1,0:T(8,128)(2,1)}, bf16[3840,128]{1,0:T(8,128)(2,1)}, bf16[3840,128]{1,0:T(8,128)(2,1)}) custom-call(s32[1]{0:T(128)} %bitcast.core_ref, s32[1,15]{1,0:T(1,128)} %bitcast.6, s32[1,15]{1,0:T(1,128)S(1)} %bitcast.4, bf16[1920,512]{1,0:T(8,128)(2,1)} %lat0_hbm.1, ...), custom_call_target="tpu_custom_call" | custom-call | flops 2013265920 | bytes 7864320 | tf_op jit(solution)/shard_map/project/pallas_call | solution.py:226
  18.4 0.0 copy-start.2
  18.4 0.0 copy-start
  18.4 0.0 copy-start.1
  18.4 0.0 all-to-all-done.q_ref
  18.4 6.6 %attend.1 = bf16[16,72,128]{2,1,0:T(8,128)(2,1)} custom-call(bf16[16,64,128]{2,1,0:T(8,128)(2,1)S(1)} %all-to-all-done.q_ref, bf16[3840,128]{1,0:T(8,128)(2,1)S(1)} %get-tuple-element.17.k0_ref, bf16[768,128]{1,0:T(8,128)(2,1)S(1)} %get-tuple-element.18.v0_ref, bf16[3072,128]{1,0:T(8,128)(2,1)} %get-tuple-element.19.v0_hbm, ...), custom_call_target="tpu_custom_call" | custom-call | flops 2013265920 | bytes 3932160 | tf_op jit(solution)/shard_map/attend/pallas_call | solution.py:353
  25.0 5.1 %all-to-all-start.1 = ((bf16[16,72,128]{2,1,0:T(8,128)(2,1)}), bf16[16,72,128]{2,1,0:T(8,128)(2,1)S(1)}, u32[]{:S(2)}, u32[]{:S(2)}) async-start(bf16[16,72,128]{2,1,0:T(8,128)(2,1)} %attend.1), calls=%async_computation.1 | async-start | bytes 589824 | tf_op jit(solution)/shard_map/all_to_all | solution.py:526
  30.2 0.0 copy-done.2
  30.2 0.0 copy-done
  30.2 0.0 copy-done.1
  30.2 6.2 %suffix.1 = (f32[128,128]{1,0:T(8,128)S(1)}, f32[128,128]{1,0:T(8,128)S(1)}, f32[128,128]{1,0:T(8,128)S(1)}) custom-call(s32[1]{0:T(128)S(6)} %copy.15.len_ref, bf16[128,128]{1,0:T(8,128)(2,1)S(1)} %copy-done, bf16[16,512]{1,0:T(8,128)(2,1)S(1)} %copy-done.1, bf16[16,512]{1,0:T(8,128)(2,1)S(1)} %pad.4.nv_ref, bf16[1,4096,512]{2,1,0:T(8,128)(2,1)} %k_ref.1, ...), custom_call_target="tpu_custom_call" | custom-call | flops 268435456 | bytes 8388608 | tf_op jit(solution)/shard_map/suffix/pallas_call | solution.py:444
  36.4 0.6 %all-to-all-done.1.got_ref = bf16[16,72,128]{2,1,0:T(8,128)(2,1)S(1)} async-done(((bf16[16,72,128]{2,1,0:T(8,128)(2,1)}), bf16[16,72,128]{2,1,0:T(8,128)(2,1)S(1)}, u32[]{:S(2)}, u32[]{:S(2)}) %all-to-all-start.1) | async-done | bytes 294944 | tf_op jit(solution)/shard_map/all_to_all | solution.py:526
  37.0 0.9 %combine.1 = bf16[1,4,4096]{2,1,0:T(4,128)(2,1)} custom-call(bf16[16,72,128]{2,1,0:T(8,128)(2,1)S(1)} %all-to-all-done.1.got_ref, f32[128,128]{1,0:T(8,128)S(1)} %get-tuple-element.24.acc_ref, f32[128,128]{1,0:T(8,128)S(1)} %get-tuple-element.25.peak_ref, f32[128,128]{1,0:T(8,128)S(1)} %get-tuple-element.26.total_ref), custom_call_target="tpu_custom_call" | custom-call | tf_op jit(solution)/shard_map/combine/pallas_call | solution.py:503
  (1 shorter events, 0.0 us)
Async XLA Ops:
  0.0 12.0 %collective-permute-start.1 = (bf16[1920,512]{1,0:T(8,128)(2,1)}, bf16[1920,512]{1,0:T(8,128)(2,1)S(1)}, u32[]{:S(2)}, u32[]{:S(2)}) collective-permute-start(bf16[1920,512]{1,0:T(8,128)(2,1)} %lat0_hbm.1), channel_id=1, source_target_pairs={{0,1},{1,0},{2,3},{3,2},{4,5},{5,4},{6,7},{7,6},{8,9},{9,8},{10,11... | collective-permute-start | bytes 5898248 | tf_op jit(solution)/shard_map/ppermute | solution.py:546
  2.7 15.7 %all-to-all-start = ((bf16[16,64,128]{2,1,0:T(8,128)(2,1)}), bf16[16,64,128]{2,1,0:T(8,128)(2,1)S(1)}, u32[]{:S(2)}, u32[]{:S(2)}) async-start(bf16[16,64,128]{2,1,0:T(8,128)(2,1)} %get-tuple-element.16), calls=%async_computation | async-start | bytes 524288 | tf_op jit(solution)/shard_map/all_to_all | solution.py:526
  10.7 1.3 %collective-permute-start = (s32[15]{0:T(128)}, s32[15]{0:T(128)S(1)}, u32[]{:S(2)}, u32[]{:S(2)}) collective-permute-start(s32[15]{0:T(128)} %param.15), channel_id=1, source_target_pairs={{0,1},{1,0},{2,3},{3,2},{4,5},{5,4},{6,7},{7,6},{8,9},{9,8},{10,11... | collective-permute-start | bytes 188 | tf_op jit(solution)/shard_map/ppermute | solution.py:547
  18.4 11.8 %copy-start.2 = (bf16[1,4,512]{2,1,0:T(4,128)(2,1)S(1)}, bf16[1,4,512]{2,1,0:T(4,128)(2,1)}, u32[]{:S(2)}) copy-start(bf16[1,4,512]{2,1,0:T(4,128)(2,1)} %param.20) | copy-start | bytes 12292
  18.4 11.8 %copy-start = (bf16[128,128]{1,0:T(8,128)(2,1)S(1)}, bf16[128,128]{1,0:T(8,128)(2,1)}, u32[]{:S(2)}) copy-start(bf16[128,128]{1,0:T(8,128)(2,1)} %get-tuple-element.22.q_ref) | copy-start | bytes 98308
  18.4 11.8 %copy-start.1 = (bf16[16,512]{1,0:T(8,128)(2,1)S(1)}, bf16[16,512]{1,0:T(8,128)(2,1)}, u32[]{:S(2)}) copy-start(bf16[16,512]{1,0:T(8,128)(2,1)} %get-tuple-element.23.nk_ref) | copy-start | bytes 49156
  25.0 12.0 %all-to-all-start.1 = ((bf16[16,72,128]{2,1,0:T(8,128)(2,1)}), bf16[16,72,128]{2,1,0:T(8,128)(2,1)S(1)}, u32[]{:S(2)}, u32[]{:S(2)}) async-start(bf16[16,72,128]{2,1,0:T(8,128)(2,1)} %attend.1), calls=%async_computation.1 | async-start | bytes 589824 | tf_op jit(solution)/shard_map/all_to_all | solution.py:526
